TPU v7x, 32 devices: a whole 2x2x4 slice. The times are simulated.
32 devices in a mesh: run: 2 (over y), team: 4 (over x, core), ma: 4 (over z).
Axes of the slice: x: 2, y: 2, z: 4, core: 2. Of those that a mesh axis runs over, the one named last changes fastest.
Arguments:
- section: bfloat16 [8, 2, 3, 24, 2, 32896], P(('run', 'team'), None, None, None, None, 'ma'), parts along dimension 0, may hold values from -6 to 6
- start: float32 [8, 2, 3, 24, 2, 32896], P(('run', 'team'), None, None, None, None, 'ma'), parts along dimension 0, may hold values from -6 to 6
- velocity: bfloat16 [768, 3, 24, 768], P(('run', 'ma'), None, 'team'), parts along dimension 0, may hold values from -6 to 6
- pair_list: int32 [128], P('ma'), may hold values from 0 to 127, each once
- wavenumber: int32 [4], P('team'), may hold values from 1 to 23
Outputs:
- updated: float32 [8, 2, 3, 24, 2, 32896], P(('run', 'team'), None, None, None, None, 'ma'), parts along dimension 0
There are 2 independent parts, one for each index of `run`. A program takes and returns all parts, laid end to end along the dimension named above; an argument that names none is the same for every part. Nothing has to cross between parts.
Inputs may be any that keep to these rules, and one draw needn't show every extreme that they name: Block q of the rows holds orders pair_list[q] and 255 - pair_list[q]; each value appears once.
All inputs are finite; a program needn't handle non-finite values.
Results may differ from a plain program's by a relative error of at most 0.0078.
Values may be sent and summed in bfloat16 or wider, within the bound.
No kernel may reach another device: no remote copies, remote signals or barrier semaphores. Data moves between devices by JAX's collectives and lax.ppermute only.
A program may use at most 320 MiB of HBM per device.

v0:
```python
import functools
import math

import jax
import jax.numpy as jnp
from jax import lax
from jax.experimental import pallas as pl
from jax.experimental.pallas import tpu as pltpu
from jax.sharding import Mesh, PartitionSpec as P

NM = 256
NLAT = 384
NLON = 768
LEV = 24
TESTS = 2


grid_scale = 1.0 / 64.0
anchor_gain = 64.0 * math.sqrt(4.0 * math.pi)
quadrature_gain = 64.0
diffusion = 7e-06
step_weight = 2.0
row_block = 16


def seed_values(order_real, order_count, sine_theta):
    factor_index = jnp.arange(1, order_count, dtype=jnp.float32)
    factor_log = jnp.log((2.0 * factor_index - 1.0) / (2.0 * factor_index))
    partial_log = jnp.sum(
        jnp.where(factor_index[None, :] <= order_real[:, None], factor_log[None, :], 0.0), axis=1
    )
    seed_log = 0.5 * (jnp.log((2.0 * order_real + 1.0) / (4.0 * jnp.pi)) + partial_log)
    return jnp.exp(seed_log[:, None] + order_real[:, None] * jnp.log(sine_theta)[None, :])


def pair_table(pair_ids, order_count, lat_count):
    pair_count = pair_ids.shape[0]
    order_low = pair_ids.astype(jnp.float32)
    order_high = (order_count - 1 - pair_ids).astype(jnp.float32)
    colatitude = jnp.pi * (jnp.arange(lat_count, dtype=jnp.float32) + 0.5) / lat_count
    cosine = jnp.cos(colatitude)
    sine_theta = jnp.sin(colatitude)
    seed_low = seed_values(order_low, order_count, sine_theta)
    seed_high = seed_values(order_high, order_count, sine_theta)
    switch_row = order_count - pair_ids

    def one_row(state_pair, row_id):
        latest, before = state_pair
        in_low = row_id < switch_row
        degree = jnp.where(in_low, pair_ids + row_id, row_id - 1)
        order_real = jnp.where(in_low, order_low, order_high)
        degree_real = degree.astype(jnp.float32)
        active = degree_real > order_real
        divisor = jnp.where(active, degree_real * degree_real - order_real * order_real, 1.0)
        upper = jnp.sqrt(jnp.maximum(4.0 * degree_real * degree_real - 1.0, 0.0) / divisor)
        lower_num = ((degree_real - 1.0) * (degree_real - 1.0) - order_real * order_real) * (
            2.0 * degree_real + 1.0
        )
        lower = jnp.sqrt(
            jnp.maximum(lower_num, 0.0) / (divisor * jnp.maximum(2.0 * degree_real - 3.0, 1.0))
        )
        recurred = upper[:, None] * cosine[None, :] * latest - lower[:, None] * before
        is_seed = (row_id == 0) | (row_id == switch_row)
        seeded = jnp.where(in_low[:, None], seed_low, seed_high)
        current = jnp.where(is_seed[:, None], seeded, jnp.where(active[:, None], recurred, 0.0))
        return ((current, latest), current)

    def block_rows(state_pair, first_row):
        produced = []
        for offset in range(row_block):
            state_pair, current = one_row(state_pair, first_row + offset)
            produced.append(current)
        return (state_pair, jnp.stack(produced))

    turns = -(-(order_count + 1) // row_block)
    blank_rows = jnp.zeros((pair_count, lat_count), jnp.float32)
    firsts = jnp.arange(turns, dtype=jnp.int32) * row_block
    _, values = lax.scan(block_rows, (blank_rows, blank_rows), firsts)
    leg_table = values.reshape(turns * row_block, pair_count, lat_count)[: order_count + 1]
    row_index = jnp.arange(order_count + 1, dtype=jnp.int32)
    first_half = row_index[None, :] < (order_count - pair_ids)[:, None]
    degree = jnp.where(first_half, pair_ids[:, None] + row_index[None, :], row_index[None, :] - 1)
    return (leg_table, first_half, degree)


def wave_table(order_list, lon_count):
    longitude = jnp.arange(lon_count, dtype=jnp.int32)
    phase_index = order_list[:, None] * longitude[None, :] % lon_count
    angle_rad = 2.0 * jnp.pi / lon_count * phase_index.astype(jnp.float32)
    return jnp.stack([jnp.cos(angle_rad), jnp.sin(angle_rad)])


def lat_weights(latitudes, lat_count):
    colatitude = jnp.pi * (latitudes.astype(jnp.float32) + 0.5) / lat_count
    return quadrature_gain * (jnp.pi / lat_count) * jnp.sin(colatitude)


def test_field(wave_index, test_count, levels):
    component = jnp.arange(3, dtype=jnp.int32)
    test_ids = jnp.arange(test_count, dtype=jnp.int32)
    level_ids = jnp.arange(levels, dtype=jnp.float32)
    aligned = (component[None, :] == test_ids[:, None]).astype(jnp.float32)
    profile = jnp.cos(jnp.pi * wave_index.astype(jnp.float32) * (level_ids + 0.5) / levels)
    return anchor_gain * aligned[:, :, None] * profile[None, None, :]


def cross_field(motion, magnetic, along):
    return jnp.roll(motion, -1, along) * jnp.roll(magnetic, -2, along) - jnp.roll(
        motion, -2, along
    ) * jnp.roll(magnetic, -1, along)


def shards_general(section, start, velocity, pair_list, wavenumber):
    pair_count = pair_list.shape[0]
    leg_table, first_half, degree = pair_table(pair_list, NM, NLAT)
    legendre = leg_table.astype(jnp.bfloat16)
    selectors = jnp.stack([first_half, jnp.logical_not(first_half)], axis=1)
    masks_low = selectors.astype(jnp.bfloat16)
    anchor = (pair_list == 0)[:, None] & (jnp.arange(NM + 1) == 0)[None, :]
    anchor_rows = anchor.reshape(-1).astype(jnp.float32)
    part_pick = jnp.array([1.0, 0.0], jnp.float32)
    forcing = test_field(wavenumber[0], TESTS, LEV)
    spec_field = (
        section[0].astype(jnp.float32)
        + forcing[:, :, :, None, None] * part_pick[:, None] * anchor_rows[None, :]
    )
    spec_field = spec_field.astype(jnp.bfloat16).reshape(TESTS, 3, LEV, 2, pair_count, NM + 1)
    masked = spec_field[:, :, :, :, :, None, :] * masks_low
    spectra = jnp.einsum(
        "scvpqhr,rqa->ascvpqh", masked, legendre, preferred_element_type=jnp.float32
    )
    spectra = spectra.astype(jnp.bfloat16).reshape(NLAT, TESTS, 3, LEV, 2, 2 * pair_count)
    every_pair = lax.all_gather(pair_list, "ma", axis=0, tiled=True)
    order_list = jnp.stack([every_pair, NM - 1 - every_pair], axis=1).reshape(-1)
    waves = wave_table(order_list, NLON)
    inverse_table = (waves * grid_scale).astype(jnp.bfloat16)
    forward_table = (waves * (2.0 * jnp.pi / NLON)).astype(jnp.bfloat16)
    wind_field = lax.all_gather(velocity, "team", axis=2, tiled=True)
    band_size = velocity.shape[0]
    latitudes = lax.axis_index("ma") * band_size + jnp.arange(band_size, dtype=jnp.int32)
    weights = lat_weights(latitudes, NLAT)
    collected = []
    for test_id in range(TESTS):
        grid_field = jnp.einsum(
            "ascvpm,pmo->ascvo",
            lax.all_to_all(
                spectra[:, test_id : test_id + 1], "ma", split_axis=0, concat_axis=5, tiled=True
            ),
            inverse_table,
            preferred_element_type=jnp.float32,
        )
        emf = cross_field(wind_field[:, None], grid_field, 2).astype(jnp.bfloat16)
        fourier = jnp.einsum(
            "ascvo,pmo->ascvpm", emf, forward_table, preferred_element_type=jnp.float32
        )
        fourier = (fourier * weights[:, None, None, None, None, None]).astype(jnp.bfloat16)
        collected.append(lax.all_to_all(fourier, "ma", split_axis=5, concat_axis=0, tiled=True))
    returned = jnp.concatenate(collected, axis=1)
    returned = returned.reshape(NLAT, TESTS, 3, LEV, 2, pair_count, 2)
    project = jnp.einsum(
        "ascvpqh,rqa->scvpqhr", returned, legendre, preferred_element_type=jnp.float32
    )
    tendency = jnp.sum(project * selectors.astype(jnp.float32), axis=5).reshape(
        TESTS, 3, LEV, 2, -1
    )
    spread = (degree * (degree + 1)).astype(jnp.float32).reshape(-1)
    updated = start[0] + step_weight * (
        tendency - diffusion * spread * section[0].astype(jnp.float32)
    )
    return updated[None]


BF16 = jnp.bfloat16
F32 = jnp.float32
VMEM_CAP = 56 << 20
PAIR_ROWS = NM + 1
CHUNK_ROWS = 16
SLOTS = 8


def work(micros):
    return pl.CostEstimate(
        flops=int(micros * 1e9), transcendentals=0, bytes_accessed=int(micros * 1e6)
    )


def after(value, *others):
    return lax.optimization_barrier((value,) + others)[0]


def table_window(slots):
    return -(-(PAIR_ROWS + slots - 1) // 32) * 32


def swap_major(block):
    return jnp.swapaxes(block, 0, 1)


def table_kernel(upper, lower, first, second, seed_low, seed_high, cosine, out, *, lead):
    shape = seed_low.shape
    cosine_rows = jnp.broadcast_to(cosine[...], shape)
    first_step = first[...]
    second_step = second[...]
    low_value = seed_low[...]
    high_value = seed_high[...]

    def chunk(starting, index, state):
        latest, before = state
        scale_up = upper[index]
        scale_down = lower[index]
        produced = []
        for offset in range(CHUNK_ROWS):
            step = index * CHUNK_ROWS + offset
            current = (scale_up[:, offset : offset + 1] * cosine_rows) * latest - scale_down[
                :, offset : offset + 1
            ] * before
            current = jnp.where(second_step == step, high_value, current)
            if starting:
                current = jnp.where(first_step == step, low_value, current)
            produced.append(current)
            latest, before = current, latest
        rows = swap_major(jnp.stack(produced))
        out[:, pl.ds(pl.multiple_of(index * CHUNK_ROWS, CHUNK_ROWS), CHUNK_ROWS), :] = rows.astype(
            BF16
        )
        return latest, before

    blank = jnp.zeros(shape, F32)
    state = lax.fori_loop(0, lead, functools.partial(chunk, True), (blank, blank))
    lax.fori_loop(lead, out.shape[1] // CHUNK_ROWS, functools.partial(chunk, False), state)


def legendre_table(every_pair, slots, lats):
    pairs = every_pair.shape[0]
    window = table_window(slots)
    order_low = every_pair.astype(F32)
    order_high = (NM - 1 - every_pair).astype(F32)
    colatitude = jnp.pi * (lats.astype(F32) + 0.5) / NLAT
    seed_low = seed_values(order_low, NM, jnp.sin(colatitude))
    seed_high = seed_values(order_high, NM, jnp.sin(colatitude))
    slot = jnp.arange(pairs, dtype=jnp.int32) % slots
    row = jnp.arange(window, dtype=jnp.int32)[None, :] - slot[:, None]
    switch = NM - every_pair
    in_low = row < switch[:, None]
    degree = jnp.where(in_low, every_pair[:, None] + row, row - 1)
    order = jnp.where(in_low, order_low[:, None], order_high[:, None])
    real = degree.astype(F32)
    active = (real > order) & (row >= 0) & (row < PAIR_ROWS)
    divisor = jnp.where(active, real * real - order * order, 1.0)
    upper = jnp.sqrt(jnp.maximum(4.0 * real * real - 1.0, 0.0) / divisor)
    lower_num = ((real - 1.0) * (real - 1.0) - order * order) * (2.0 * real + 1.0)
    lower = jnp.sqrt(
        jnp.maximum(lower_num, 0.0) / (divisor * jnp.maximum(2.0 * real - 3.0, 1.0))
    )
    by_chunk = lambda values: jnp.swapaxes(
        jnp.where(active, values, 0.0).reshape(pairs, window // CHUNK_ROWS, CHUNK_ROWS), 0, 1
    )
    lanes = lats.shape[0]
    spread_out = lambda values: jnp.broadcast_to(values[:, None], (pairs, lanes))
    chunks = window // CHUNK_ROWS
    coefficient = pl.BlockSpec((chunks, 8, CHUNK_ROWS), lambda q: (0, q, 0))
    per_pair = pl.BlockSpec((8, lanes), lambda q: (q, 0))
    lead = -(-slots // CHUNK_ROWS)
    return pl.pallas_call(
        functools.partial(table_kernel, lead=lead),
        grid=(pairs // 8,),
        in_specs=[coefficient, coefficient, per_pair, per_pair, per_pair, per_pair]
        + [pl.BlockSpec((1, lanes), lambda q: (0, 0))],
        out_specs=pl.BlockSpec((8, window, lanes), lambda q: (q, 0, 0)),
        out_shape=jax.ShapeDtypeStruct((pairs, window, lanes), BF16),
        compiler_params=pltpu.CompilerParams(vmem_limit_bytes=VMEM_CAP),
        cost_estimate=work(40),
        name="table",
    )(
        by_chunk(upper),
        by_chunk(lower),
        spread_out(slot),
        spread_out(slot + switch),
        seed_low,
        seed_high,
        jnp.cos(colatitude)[None, :],
    )


def row_mask(switch, source, place, slots, lane):
    turn = switch[source * slots + place]
    in_low = lane < turn
    even = ((lane - jnp.where(in_low, place, turn)) & 1) == 0
    anchor = (lane == place) & (turn == place + NM)
    return in_low, even, anchor


def mirror_sign(fields):
    lane = lax.broadcasted_iota(jnp.int32, (fields, 128), 1)
    return jnp.where(lane < 64, 1.0, -1.0).astype(F32)


def synthesis_kernel(switch, spec, table, forcing, out, *, slots):
    source = pl.program_id(0)
    window = table.shape[1]
    pieces = spec.shape[2]
    fields = 4 * pieces
    sign = mirror_sign(fields)
    lane = lax.broadcasted_iota(jnp.int32, (fields, window), 1)
    force = jnp.broadcast_to(forcing[...], (fields, window))

    def group(index, _):
        collected = []
        for slot in range(SLOTS):
            place = index * SLOTS + slot
            in_low, even, anchor = row_mask(switch, source, place, slots, lane)
            span = pl.ds(pl.multiple_of(place * NM, NM), window)
            rows = jnp.concatenate(
                [
                    spec[team, 0, piece, :, span].astype(F32)
                    for team in range(2)
                    for piece in range(pieces)
                ],
                axis=0,
            )
            rows = rows + jnp.where(anchor, force, 0.0)
            low, high = jnp.where(in_low, rows, 0.0), jnp.where(in_low, 0.0, rows)
            split = [
                jnp.where(even, low, 0.0),
                jnp.where(even, 0.0, low),
                jnp.where(even, high, 0.0),
                jnp.where(even, 0.0, high),
            ]
            made = jnp.dot(
                jnp.concatenate(split, axis=0).astype(BF16),
                table[place],
                preferred_element_type=F32,
            )
            for order in range(2):
                same = made[2 * order * fields : (2 * order + 1) * fields]
                flips = made[(2 * order + 1) * fields : (2 * order + 2) * fields]
                collected.append(
                    jnp.concatenate(
                        [
                            same[:, :128] + flips[:, :128],
                            same[:, :128] - flips[:, :128],
                            same[:, 128:] + sign * flips[:, 128:],
                        ],
                        axis=1,
                    )
                )
        rows = pl.ds(pl.multiple_of(index * 2 * SLOTS, 2 * SLOTS), 2 * SLOTS)
        out[:, rows, :] = swap_major(jnp.stack(collected)).astype(BF16)
        return 0

    lax.fori_loop(0, slots // SLOTS, group, 0)


def synthesis(spec, table, forcing, switch, slots):
    _, sources, pieces, parts, width = spec.shape
    fields = 2 * pieces * parts
    pairs, window, lanes = table.shape
    return pl.pallas_call(
        functools.partial(synthesis_kernel, slots=slots),
        grid_spec=pltpu.PrefetchScalarGridSpec(
            num_scalar_prefetch=1,
            grid=(sources,),
            in_specs=[
                pl.BlockSpec((2, 1, pieces, parts, width), lambda z, _: (0, z, 0, 0, 0)),
                pl.BlockSpec((slots, window, lanes), lambda z, _: (z, 0, 0)),
                pl.BlockSpec((fields, 1), lambda z, _: (0, 0)),
            ],
            out_specs=pl.BlockSpec((fields, 2 * slots, NLAT), lambda z, _: (0, z, 0)),
        ),
        out_shape=jax.ShapeDtypeStruct((fields, 2 * pairs, NLAT), BF16),
        compiler_params=pltpu.CompilerParams(vmem_limit_bytes=VMEM_CAP),
        cost_estimate=work(14),
        name="synthesis",
    )(switch, spec, table, forcing)


LON_TILE = 256


def grid_kernel(
    spectra, first, second, arrange, inverse_cos, inverse_sin, forward_cos, forward_sin, weights,
    out, wind, emf,
):
    @pl.when(pl.program_id(0) == 0)
    def _():
        for c in range(3):
            bands = [
                half[z, c] for z in range(first.shape[0]) for half in (first, second)
            ]
            wind[c] = lax.dot_general(
                jnp.concatenate(bands, axis=0),
                arrange[...],
                (((0,), (0,)), ((), ())),
                preferred_element_type=F32,
            ).astype(BF16)

    for tile in range(NLON // LON_TILE):
        span = pl.ds(tile * LON_TILE, LON_TILE)
        magnetic = [
            jnp.dot(inverse_cos[span, :], spectra[2 * c], preferred_element_type=F32)
            + jnp.dot(inverse_sin[span, :], spectra[2 * c + 1], preferred_element_type=F32)
            for c in range(3)
        ]
        motion = [wind[c, span, :].astype(F32) for c in range(3)]
        for c in range(3):
            one, two = (c + 1) % 3, (c + 2) % 3
            emf[c, span, :] = (
                motion[one] * magnetic[two] - motion[two] * magnetic[one]
            ).astype(BF16)
    scale = weights[...]
    for c in range(3):
        for part, table in enumerate((forward_cos, forward_sin)):
            back = jnp.dot(table[...], emf[c], preferred_element_type=F32)
            out[2 * c + part] = (back * scale).astype(BF16)


def grid_product(spectra, first, second, arrange, tables, weights):
    fields, orders, lats = spectra.shape
    whole = lambda array: pl.BlockSpec(array.shape, lambda g: (0,) * array.ndim)
    per_group = pl.BlockSpec((6, orders, lats), lambda g: (g, 0, 0))
    fixed = (first, second, arrange) + tuple(tables) + (weights,)
    return pl.pallas_call(
        grid_kernel,
        grid=(fields // 6,),
        in_specs=[per_group] + [whole(array) for array in fixed],
        out_specs=per_group,
        out_shape=jax.ShapeDtypeStruct(spectra.shape, BF16),
        scratch_shapes=[pltpu.VMEM((3, NLON, lats), BF16)] * 2,
        compiler_params=pltpu.CompilerParams(vmem_limit_bytes=VMEM_CAP),
        cost_estimate=work(16),
        name="grid_product",
    )(spectra, *fixed)


def analysis_kernel(switch, fourier, table, out, *, slots):
    source = pl.program_id(0)
    window = table.shape[1]
    fields = fourier.shape[0]
    pieces = out.shape[2]
    width = out.shape[4]
    sign = mirror_sign(fields)
    lane = lax.broadcasted_iota(jnp.int32, (fields, window), 1)
    blank = jnp.zeros((fields, 128 - (window - NM)), F32)

    def store(values, span):
        for team in range(2):
            for piece in range(pieces):
                row = 2 * (team * pieces + piece)
                out[team, 0, piece, :, span] = values[row : row + 2].astype(BF16)

    def group(index, over):
        rows = pl.ds(pl.multiple_of(index * 2 * SLOTS, 2 * SLOTS), 2 * SLOTS)
        by_order = swap_major(fourier[:, rows, :].astype(F32))
        for slot in range(SLOTS):
            place = index * SLOTS + slot
            in_low, even, _ = row_mask(switch, source, place, slots, lane)
            split = []
            for order in range(2):
                values = by_order[2 * slot + order]
                north, south, rest = values[:, :128], values[:, 128:256], values[:, 256:]
                split += [
                    jnp.concatenate([north + south, rest], axis=1),
                    jnp.concatenate([north - south, rest * sign], axis=1),
                ]
            made = lax.dot_general(
                jnp.concatenate(split, axis=0).astype(BF16),
                table[place],
                (((1,), (1,)), ((), ())),
                preferred_element_type=F32,
            )
            part = [made[k * fields : (k + 1) * fields] for k in range(4)]
            made = jnp.where(
                in_low, jnp.where(even, part[0], part[1]), jnp.where(even, part[2], part[3])
            )
            start = pl.multiple_of(place * NM, NM)
            store(
                jnp.concatenate([made[:, :128] + over, made[:, 128:NM]], axis=1),
                pl.ds(start, NM),
            )
            over = jnp.concatenate([made[:, NM:], blank], axis=1)
        return over

    over = lax.fori_loop(0, slots // SLOTS, group, jnp.zeros((fields, 128), F32))
    full = slots * NM
    store(over[:, : width - full], pl.ds(full, width - full))


def analysis(fourier, table, switch, slots, width):
    fields, orders, lats = fourier.shape
    pairs, window, lanes = table.shape
    sources = pairs // slots
    pieces = fields // 4
    return pl.pallas_call(
        functools.partial(analysis_kernel, slots=slots),
        grid_spec=pltpu.PrefetchScalarGridSpec(
            num_scalar_prefetch=1,
            grid=(sources,),
            in_specs=[
                pl.BlockSpec((fields, 2 * slots, NLAT), lambda z, _: (0, z, 0)),
                pl.BlockSpec((slots, window, lanes), lambda z, _: (z, 0, 0)),
            ],
            out_specs=pl.BlockSpec((2, 1, pieces, 2, width), lambda z, _: (0, z, 0, 0, 0)),
        ),
        out_shape=jax.ShapeDtypeStruct((2, sources, pieces, 2, width), BF16),
        compiler_params=pltpu.CompilerParams(vmem_limit_bytes=VMEM_CAP),
        cost_estimate=work(14),
        name="analysis",
    )(switch, fourier, table)


def pack_kernel(section, out):
    out[0] = section[:, 0, 0]


def pack_level(section, level):
    pieces, targets, _, parts, width = section.shape
    return pl.pallas_call(
        pack_kernel,
        grid=(targets,),
        in_specs=[pl.BlockSpec((pieces, 1, 1, parts, width), lambda d: (0, d, level, 0, 0))],
        out_specs=pl.BlockSpec((1, pieces, parts, width), lambda d: (d, 0, 0, 0)),
        out_shape=jax.ShapeDtypeStruct((targets, pieces, parts, width), BF16),
        cost_estimate=work(5),
        name="pack",
    )(section)


def finish_kernel(base, tendency, out):
    fields = tendency.shape[2]
    for field in range(fields):
        out[0, field, :, :, 0] = base[0, field, :, :, 0] + step_weight * tendency[
            :, :, field
        ].astype(F32)


def finish(total, tendency, level):
    tests, comps, teams, count, depth, parts, width = total.shape
    own = pl.BlockSpec(
        (1, comps, teams, count, 1, parts, width), lambda s: (s, 0, 0, 0, level, 0, 0)
    )
    return pl.pallas_call(
        finish_kernel,
        grid=(tests,),
        in_specs=[
            own,
            pl.BlockSpec((teams, count, comps, parts, width), lambda s: (0, 0, s, 0, 0)),
        ],
        out_specs=own,
        out_shape=jax.ShapeDtypeStruct(total.shape, F32),
        input_output_aliases={0: 0},
        compiler_params=pltpu.CompilerParams(vmem_limit_bytes=VMEM_CAP),
        cost_estimate=work(5),
        name="finish",
    )(total, tendency)


def gather_pairs(pair_list, count):
    own = pair_list.shape[0]
    place = lax.axis_index("ma")
    every = jnp.zeros((count, own), jnp.int32)
    every = lax.dynamic_update_slice(every, pair_list[None], (place, 0))
    for shift in range(1, count):
        moved = lax.ppermute(pair_list, "ma", [(k, (k + shift) % count) for k in range(count)])
        every = lax.dynamic_update_slice(every, moved[None], ((place - shift) % count, 0))
    return every.reshape(-1)


def shards_by_level(section, start, velocity, pair_list, wavenumber, *, count):
    slots = pair_list.shape[0]
    width = section.shape[-1]
    depth = LEV // (2 * count)
    band = velocity.shape[0]
    half = band // 2
    place = lax.axis_index("ma")
    across = lax.axis_index("x")
    core = lax.axis_index("k")
    swap_cores = [(0, 1), (1, 0)]
    every_pair = gather_pairs(pair_list, count)
    slot_of = jnp.arange(count * slots, dtype=jnp.int32) % slots
    switch = slot_of + NM - every_pair

    other = lax.ppermute(wavenumber, "k", swap_cores)
    waves_here = jnp.where(core == 0, jnp.stack([wavenumber, other]), jnp.stack([other, wavenumber]))
    forcing = jnp.stack([test_field(waves_here[team, 0], TESTS, LEV) for team in range(2)])
    forcing = forcing.reshape(2 * TESTS * 3, LEV)
    forcing = lax.dynamic_slice_in_dim(forcing, (core * count + place) * depth, depth, axis=1)
    forcing = jnp.stack([forcing, jnp.zeros_like(forcing)], axis=1).reshape(-1, depth)

    by_level = section.reshape(TESTS * 3, 2 * count, depth, 2, width)
    exchange = functools.partial(
        lax.all_to_all, axis_name=("k", "ma"), split_axis=0, concat_axis=0, tiled=True
    )
    sent = pack_level(by_level, 0)
    arrived = exchange(sent)
    specs = [arrived]

    bands = after(velocity, sent).reshape(2, half, 3, LEV // 4, NLON).transpose(0, 3, 2, 1, 4)
    mine = lax.dynamic_index_in_dim(bands, core, 0, keepdims=False)
    theirs = lax.dynamic_index_in_dim(bands, 1 - core, 0, keepdims=False)
    theirs = lax.ppermute(theirs, "k", swap_cores)
    split = jnp.where(core == 0, jnp.stack([mine, theirs]), jnp.stack([theirs, mine]))
    split = split.reshape(count, depth, 3, half, NLON)

    mid = NLAT // 2
    north = jnp.arange(mid, dtype=jnp.int32)
    lats = jnp.concatenate(
        [north[:128], NLAT - 1 - north[:128], north[128:], NLAT - 1 - north[128:]]
    )
    arrange = (jnp.arange(NLAT, dtype=jnp.int32)[:, None] == lats[None, :]).astype(BF16)
    table = legendre_table(every_pair, slots, jnp.concatenate([north, north[128:]]))
    order_list = jnp.stack([every_pair, NM - 1 - every_pair], axis=1).reshape(-1)
    waves = wave_table(order_list, NLON)
    inverse_table = (waves * grid_scale).astype(BF16)
    forward_table = (waves * (2.0 * jnp.pi / NLON)).astype(BF16)
    tables = (inverse_table[0].T, inverse_table[1].T, forward_table[0], forward_table[1])
    weights = lat_weights(lats, NLAT)[None, :]

    row_index = jnp.arange(PAIR_ROWS, dtype=jnp.int32)
    first_half = row_index[None, :] < (NM - pair_list)[:, None]
    degree = jnp.where(first_half, pair_list[:, None] + row_index[None, :], row_index[None, :] - 1)
    spread = (degree * (degree + 1)).astype(F32).reshape(-1)
    total = start[0] - (step_weight * diffusion) * spread * section[0].astype(F32)
    total = total.reshape(TESTS, 3, 2, count, depth, 2, width)

    own_first = (across == 0) & (core == 0)
    own_second = (across == 1) & (core == 1)

    held = lax.all_to_all(
        after(split, arrived, table), "ma", split_axis=0, concat_axis=0, tiled=True
    )
    winds = []
    last = ()
    for group in (slice(0, 1), slice(1, depth)):
        part = after(held[:, group], *last)
        turn = lax.ppermute(part, ("x", "k"), [(0, 2), (1, 0), (2, 3), (3, 1)])
        cross = lax.ppermute(part, ("x", "k"), [(1, 2), (2, 1)])
        first = jnp.where(own_first, part, jnp.where((across == 0) & (core == 1), cross, turn))
        second = jnp.where(own_second, part, jnp.where((across == 1) & (core == 0), cross, turn))
        winds += [(first[:, k], second[:, k]) for k in range(first.shape[1])]
        last = (turn, cross)

    last = (held,)
    for level in range(1, depth):
        specs.append(exchange(after(pack_level(by_level, level), *last)))
        last = (specs[-1],)
    specs = [spec.reshape(2, count, TESTS * 3, 2, width) for spec in specs]

    for level in range(depth):
        spectra = synthesis(specs[level], table, forcing[:, level : level + 1], switch, slots)
        fourier = grid_product(spectra, *winds[level], arrange, tables, weights)
        tendency = analysis(fourier, table, switch, slots, width)
        back = exchange(after(tendency.reshape(2 * count, TESTS * 3, 2, width), *last))
        last = (back,)
        total = finish(total, back.reshape(2, count, TESTS * 3, 2, width), level)
    return total.reshape(start.shape)


def solution(mesh):
    sizes = dict(mesh.shape)
    count = sizes["ma"]
    whole_slots = (NM // 2) % (count * SLOTS) == 0
    if sizes["team"] == 4 and LEV % (2 * count) == 0 and whole_slots:
        grid = Mesh(
            mesh.devices.reshape(sizes["run"], 2, 2, count), ("run", "x", "k", "ma")
        )
        team = ("x", "k")
        body = lambda *arrays: shards_by_level(*arrays, count=count)
    else:
        grid, team, body = mesh, ("team",), shards_general
    placed = (
        P(("run",) + team, None, None, None, None, "ma"),
        P(("run",) + team, None, None, None, None, "ma"),
        P(("run", "ma"), None, team, None),
        P("ma"),
        P(team),
    )
    return jax.shard_map(
        body,
        mesh=grid,
        in_specs=placed,
        out_specs=P(("run",) + team, None, None, None, None, "ma"),
        check_vma=False,
    )
```

profile of v0, /device:TPU:0, one launch (start us, length us, event | category | flops | bytes accessed | tf_op | source)
XLA Modules:
  0.0 367.9 jit_solution(10423285131281036705)
XLA Ops:
  7.0 5.4 %pack.3 = bf16[8,6,2,8224]{3,2,1,0:T(2,128)(2,1)} custom-call(bf16[6,8,3,2,8224]{4,3,2,1,0:T(2,128)(2,1)} %bitcast.75), custom_call_target="tpu_custom_call" | custom-call | flops 5000000000 | bytes 5000000 | tf_op jit(solution)/shard_map/pack/pallas_call | solution.py:517
  28.8 40.3 %table.1 = bf16[128,288,256]{2,1,0:T(8,128)(2,1)} custom-call(f32[18,128,16]{2,1,0:T(8,128)} %get-tuple-element.40.upper, f32[18,128,16]{2,1,0:T(8,128)} %get-tuple-element.39.lower, s32[128,256]{1,0:T(8,128)} %broadcast_in_dim.65.first, s32[128,256]{1,0:T(8,128)} %broadcast_in_dim.66.second, f32[128,256]{1,0:T(8,128)} %get-tuple-element.59.seed_low, ...), custom_call_target="tpu_custom_call" | custom-call | flops 40000000000 | bytes 40000000 | tf_op jit(solution)/shard_map/table/pallas_call | solution.py:264
  73.9 5.0 %all-to-all-start.1 = ((bf16[4,3,3,48,768]{4,3,2,1,0:T(8,128)(2,1)}), bf16[4,3,3,48,768]{4,3,2,1,0:T(8,128)(2,1)S(1)}, u32[]{:S(2)}, u32[]{:S(2)}) async-start(bf16[4,3,3,48,768]{4,3,2,1,0:T(8,128)(2,1)} %bitcast.70), calls=%async_computation.1 | async-start | bytes 5308416 | tf_op jit(solution)/shard_map/all_to_all | solution.py:628
  80.3 5.4 %pack.5 = bf16[8,6,2,8224]{3,2,1,0:T(2,128)(2,1)} custom-call(bf16[6,8,3,2,8224]{4,3,2,1,0:T(2,128)(2,1)} %bitcast.76), custom_call_target="tpu_custom_call" | custom-call | flops 5000000000 | bytes 5000000 | tf_op jit(solution)/shard_map/pack/pallas_call | solution.py:517
  85.7 5.4 %pack.4 = bf16[8,6,2,8224]{3,2,1,0:T(2,128)(2,1)} custom-call(bf16[6,8,3,2,8224]{4,3,2,1,0:T(2,128)(2,1)} %bitcast.77), custom_call_target="tpu_custom_call" | custom-call | flops 5000000000 | bytes 5000000 | tf_op jit(solution)/shard_map/pack/pallas_call | solution.py:517
  104.2 35.1 %all-to-all-done.1 = bf16[4,3,3,48,768]{4,3,2,1,0:T(8,128)(2,1)S(1)} async-done(((bf16[4,3,3,48,768]{4,3,2,1,0:T(8,128)(2,1)}), bf16[4,3,3,48,768]{4,3,2,1,0:T(8,128)(2,1)S(1)}, u32[]{:S(2)}, u32[]{:S(2)}) %all-to-all-start.1) | async-done | bytes 2654240 | tf_op jit(solution)/shard_map/all_to_all | solution.py:628
  142.8 4.3 %all-to-all-start.2 = ((bf16[8,6,2,8224]{3,2,1,0:T(2,128)(2,1)}), bf16[8,6,2,8224]{3,2,1,0:T(2,128)(2,1)}, u32[]{:S(2)}, u32[]{:S(2)}) async-start(bf16[8,6,2,8224]{3,2,1,0:T(2,128)(2,1)} %pack.5), calls=%async_computation.2 | async-start | bytes 3194880 | tf_op jit(solution)/shard_map/all_to_all | solution.py:644
  147.1 14.0 %synthesis.3.spectra = bf16[24,256,384]{2,1,0:T(8,128)(2,1)} custom-call(s32[128]{0:T(128)} %get-tuple-element.66.switch, bf16[2,4,6,2,8224]{4,3,2,1,0:T(2,128)(2,1)} %bitcast.80, bf16[128,288,256]{2,1,0:T(8,128)(2,1)} %table.1, f32[24,1]{1,0:T(8,128)} %get-tuple-element.43.forcing), custom_call_target="tpu_custom_call" | custom-call | flops 14000000000 | bytes 14000000 | tf_op jit(solution)/shard_map/synthesis/pallas_call | solution.py:358
  170.0 16.2 %grid_product.3.fourier = bf16[24,256,384]{2,1,0:T(8,128)(2,1)} custom-call(bf16[24,256,384]{2,1,0:T(8,128)(2,1)} %synthesis.3.spectra, bf16[4,3,48,768]{3,2,1,0:T(8,128)(2,1)} %get-tuple-element.26.first, bf16[4,3,48,768]{3,2,1,0:T(8,128)(2,1)} %get-tuple-element.25.second, bf16[384,384]{1,0:T(8,128)(2,1)} %fusion.33.arrange, ...), custom_call_target="tpu_custom_call" | custom-call | flops 16000000000 | bytes 16000000 | tf_op jit(solution)/shard_map/grid_product/pallas_call | solution.py:422
  186.2 3.6 all-to-all-start.3
  189.8 14.0 %analysis.3 = bf16[2,4,6,2,8224]{4,3,2,1,0:T(2,128)(2,1)} custom-call(s32[128]{0:T(128)} %get-tuple-element.66.switch, bf16[24,256,384]{2,1,0:T(8,128)(2,1)} %grid_product.3.fourier, bf16[128,288,256]{2,1,0:T(8,128)(2,1)} %table.1), custom_call_target="tpu_custom_call" | custom-call | flops 14000000000 | bytes 14000000 | tf_op jit(solution)/shard_map/analysis/pallas_call | solution.py:493
  210.1 14.0 %synthesis.4.spectra = bf16[24,256,384]{2,1,0:T(8,128)(2,1)} custom-call(s32[128]{0:T(128)} %get-tuple-element.66.switch, bf16[2,4,6,2,8224]{4,3,2,1,0:T(2,128)(2,1)} %bitcast.34.spec, bf16[128,288,256]{2,1,0:T(8,128)(2,1)} %table.1, f32[24,1]{1,0:T(8,128)} %get-tuple-element.42.forcing), custom_call_target="tpu_custom_call" | custom-call | flops 14000000000 | bytes 14000000 | tf_op jit(solution)/shard_map/synthesis/pallas_call | solution.py:358
  232.3 16.2 %grid_product.4.fourier = bf16[24,256,384]{2,1,0:T(8,128)(2,1)} custom-call(bf16[24,256,384]{2,1,0:T(8,128)(2,1)} %synthesis.4.spectra, bf16[4,3,48,768]{3,2,1,0:T(8,128)(2,1)} %get-tuple-element.32.first, bf16[4,3,48,768]{3,2,1,0:T(8,128)(2,1)} %get-tuple-element.30.second, bf16[384,384]{1,0:T(8,128)(2,1)} %fusion.33.arrange, ...), custom_call_target="tpu_custom_call" | custom-call | flops 16000000000 | bytes 16000000 | tf_op jit(solution)/shard_map/grid_product/pallas_call | solution.py:422
  248.5 13.9 %analysis.4 = bf16[2,4,6,2,8224]{4,3,2,1,0:T(2,128)(2,1)} custom-call(s32[128]{0:T(128)} %get-tuple-element.66.switch, bf16[24,256,384]{2,1,0:T(8,128)(2,1)} %grid_product.4.fourier, bf16[128,288,256]{2,1,0:T(8,128)(2,1)} %table.1), custom_call_target="tpu_custom_call" | custom-call | flops 14000000000 | bytes 14000000 | tf_op jit(solution)/shard_map/analysis/pallas_call | solution.py:493
  262.5 14.0 %synthesis.5.spectra = bf16[24,256,384]{2,1,0:T(8,128)(2,1)} custom-call(s32[128]{0:T(128)} %get-tuple-element.66.switch, bf16[2,4,6,2,8224]{4,3,2,1,0:T(2,128)(2,1)} %bitcast.81, bf16[128,288,256]{2,1,0:T(8,128)(2,1)} %table.1, f32[24,1]{1,0:T(8,128)} %get-tuple-element.41.forcing), custom_call_target="tpu_custom_call" | custom-call | flops 14000000000 | bytes 14000000 | tf_op jit(solution)/shard_map/synthesis/pallas_call | solution.py:358
  277.6 5.0 %all-to-all-start.5 = ((bf16[8,6,2,8224]{3,2,1,0:T(2,128)(2,1)}), bf16[8,6,2,8224]{3,2,1,0:T(2,128)(2,1)S(1)}, u32[]{:S(2)}, u32[]{:S(2)}) async-start(bf16[8,6,2,8224]{3,2,1,0:T(2,128)(2,1)} %bitcast.83), calls=%async_computation.5 | async-start | bytes 3194880 | tf_op jit(solution)/shard_map/all_to_all | solution.py:652
  282.6 16.2 %grid_product.5.fourier = bf16[24,256,384]{2,1,0:T(8,128)(2,1)} custom-call(bf16[24,256,384]{2,1,0:T(8,128)(2,1)} %synthesis.5.spectra, bf16[4,3,48,768]{3,2,1,0:T(8,128)(2,1)} %get-tuple-element.31.first, bf16[4,3,48,768]{3,2,1,0:T(8,128)(2,1)} %get-tuple-element.29.second, bf16[384,384]{1,0:T(8,128)(2,1)} %fusion.33.arrange, ...), custom_call_target="tpu_custom_call" | custom-call | flops 16000000000 | bytes 16000000 | tf_op jit(solution)/shard_map/grid_product/pallas_call | solution.py:422
  298.8 13.9 %analysis.5 = bf16[2,4,6,2,8224]{4,3,2,1,0:T(2,128)(2,1)} custom-call(s32[128]{0:T(128)} %get-tuple-element.66.switch, bf16[24,256,384]{2,1,0:T(8,128)(2,1)} %grid_product.5.fourier, bf16[128,288,256]{2,1,0:T(8,128)(2,1)} %table.1), custom_call_target="tpu_custom_call" | custom-call | flops 14000000000 | bytes 14000000 | tf_op jit(solution)/shard_map/analysis/pallas_call | solution.py:493
  312.7 7.8 %all-to-all-done.5 = bf16[8,6,2,8224]{3,2,1,0:T(2,128)(2,1)S(1)} async-done(((bf16[8,6,2,8224]{3,2,1,0:T(2,128)(2,1)}), bf16[8,6,2,8224]{3,2,1,0:T(2,128)(2,1)S(1)}, u32[]{:S(2)}, u32[]{:S(2)}) %all-to-all-start.5) | async-done | bytes 1579040 | tf_op jit(solution)/shard_map/all_to_all | solution.py:652
  325.3 10.1 %fusion.base = f32[2,3,2,4,3,2,8224]{6,5,4,3,2,1,0:T(2,128)} fusion(f32[2,3,2,4,3,2,8224]{6,5,4,3,2,1,0:T(2,128)} %bitcast.71, bf16[2,3,2,4,3,2,8224]{6,5,4,3,2,1,0:T(2,128)(2,1)} %bitcast.78, f32[8224]{0:T(1024)S(1)} %copy-done.5), kind=kLoop, calls=%fused_computation.1 | loop fusion | flops 7105536 | bytes 23718016 | tf_op jit(solution)/shard_map/sub | solution.py:622
  335.4 3.7 finish.3.base
  339.0 3.7 finish.4.base
  342.7 20.4 %all-to-all-done.6 = bf16[8,6,2,8224]{3,2,1,0:T(2,128)(2,1)S(1)} async-done(((bf16[8,6,2,8224]{3,2,1,0:T(2,128)(2,1)}), bf16[8,6,2,8224]{3,2,1,0:T(2,128)(2,1)S(1)}, u32[]{:S(2)}, u32[]{:S(2)}) %all-to-all-start.6) | async-done | bytes 1579040 | tf_op jit(solution)/shard_map/all_to_all | solution.py:652
  364.3 3.7 finish.5
  (104 shorter events, 74.7 us)
Async XLA Ops:
  0.0 22.1 %collective-permute-start = (s32[32]{0:T(128)}, s32[32]{0:T(128)S(1)}, u32[]{:S(2)}, u32[]{:S(2)}) collective-permute-start(s32[32]{0:T(128)} %param.8), channel_id=1, source_target_pairs={{0,1},{1,2},{2,3},{3,0},{4,5},{5,6},{6,7},{7,4},{8,9},{9,10},{10,1... | collective-permute-start | bytes 392 | tf_op jit(solution)/shard_map/ppermute | solution.py:563
  3.0 19.1 %collective-permute-start.1 = (s32[32]{0:T(128)}, s32[32]{0:T(128)S(1)}, u32[]{:S(2)}, u32[]{:S(2)}) collective-permute-start(s32[32]{0:T(128)} %param.8), channel_id=1, source_target_pairs={{0,2},{1,3},{2,0},{3,1},{4,6},{5,7},{6,4},{7,5},{8,10},{9,11},{10,... | collective-permute-start | bytes 392 | tf_op jit(solution)/shard_map/ppermute | solution.py:563
  5.6 16.6 %collective-permute-start.2 = (s32[32]{0:T(128)}, s32[32]{0:T(128)S(1)}, u32[]{:S(2)}, u32[]{:S(2)}) collective-permute-start(s32[32]{0:T(128)} %param.8), channel_id=1, source_target_pairs={{0,3},{1,0},{2,1},{3,2},{4,7},{5,4},{6,5},{7,6},{8,11},{9,8},{10,9... | collective-permute-start | bytes 392 | tf_op jit(solution)/shard_map/ppermute | solution.py:563
  12.4 60.3 %all-to-all-start = ((bf16[8,6,2,8224]{3,2,1,0:T(2,128)(2,1)}), bf16[8,6,2,8224]{3,2,1,0:T(2,128)(2,1)S(1)}, u32[]{:S(2)}, u32[]{:S(2)}) async-start(bf16[8,6,2,8224]{3,2,1,0:T(2,128)(2,1)} %pack.3), calls=%async_computation | async-start | bytes 3194880 | tf_op jit(solution)/shard_map/all_to_all | solution.py:594
  16.0 4.2 %copy-start.6 = (s32[32]{0:T(128)S(1)}, s32[32]{0:T(128)}, u32[]{:S(2)}) copy-start(s32[32]{0:T(128)} %param.8) | copy-start | bytes 388
  19.0 50.1 %collective-permute-start.4 = (bf16[6,3,48,768]{3,2,0,1:T(8,128)(2,1)}, bf16[6,3,48,768]{3,2,0,1:T(8,128)(2,1)}, u32[]{:S(2)}, u32[]{:S(2)}) collective-permute-start(bf16[6,3,48,768]{3,2,0,1:T(8,128)(2,1)} %get-tuple-element.28), channel_id=1, source_target_pairs={{0,4},{4,0},{1,5},{5,1},{2,6},{6,2},{3,7},{7,3},{8,12},{12,8},{9,1... | collective-permute-start | bytes 3981320 | tf_op jit(solution)/shard_map/ppermute | solution.py:600
  19.4 71.8 %collective-permute-start.3 = (s32[1]{0:T(128)}, s32[1]{0:T(128)}, u32[]{:S(2)}, u32[]{:S(2)}) collective-permute-start(s32[1]{0:T(128)} %param.9), channel_id=1, source_target_pairs={{0,4},{4,0},{1,5},{5,1},{2,6},{6,2},{3,7},{7,3},{8,12},{12,8},{9,1... | collective-permute-start | bytes 20 | tf_op jit(solution)/shard_map/ppermute | solution.py:582
  72.7 1.2 copy-start.3
  73.9 65.4 %all-to-all-start.1 = ((bf16[4,3,3,48,768]{4,3,2,1,0:T(8,128)(2,1)}), bf16[4,3,3,48,768]{4,3,2,1,0:T(8,128)(2,1)S(1)}, u32[]{:S(2)}, u32[]{:S(2)}) async-start(bf16[4,3,3,48,768]{4,3,2,1,0:T(8,128)(2,1)} %bitcast.70), calls=%async_computation.1 | async-start | bytes 5308416 | tf_op jit(solution)/shard_map/all_to_all | solution.py:628
  139.4 22.0 %collective-permute-start.5 = (bf16[4,1,3,48,768]{4,3,2,0,1:T(8,128)(2,1)S(1)}, bf16[4,1,3,48,768]{4,3,2,0,1:T(8,128)(2,1)}, u32[]{:S(2)}, u32[]{:S(2)}) collective-permute-start(bf16[4,1,3,48,768]{4,3,2,0,1:T(8,128)(2,1)S(1)} %slice_bitcast_fusion.4), channel_id=1, source_target_pairs={{4,8},{8,4},{5,9},{9,5},{6,10},{10,6},{7,11},{11,7},{20,24},{24,20... | collective-permute-start | bytes 2654216 | tf_op jit(solution)/shard_map/ppermute | solution.py:636
  141.0 21.3 %collective-permute-start.6 = (bf16[4,1,3,48,768]{4,3,2,0,1:T(8,128)(2,1)S(1)}, bf16[4,1,3,48,768]{4,3,2,0,1:T(8,128)(2,1)}, u32[]{:S(2)}, u32[]{:S(2)}) collective-permute-start(bf16[4,1,3,48,768]{4,3,2,0,1:T(8,128)(2,1)S(1)} %slice_bitcast_fusion.4), channel_id=1, source_target_pairs={{0,8},{4,0},{8,12},{12,4},{1,9},{5,1},{9,13},{13,5},{2,10},{6,2},{... | collective-permute-start | bytes 2654216 | tf_op jit(solution)/shard_map/ppermute | solution.py:635
  142.8 43.4 %all-to-all-start.2 = ((bf16[8,6,2,8224]{3,2,1,0:T(2,128)(2,1)}), bf16[8,6,2,8224]{3,2,1,0:T(2,128)(2,1)}, u32[]{:S(2)}, u32[]{:S(2)}) async-start(bf16[8,6,2,8224]{3,2,1,0:T(2,128)(2,1)} %pack.5), calls=%async_computation.2 | async-start | bytes 3194880 | tf_op jit(solution)/shard_map/all_to_all | solution.py:644
  162.2 41.5 %collective-permute-start.7 = (bf16[4,2,3,48,768]{4,3,2,0,1:T(8,128)(2,1)S(1)}, bf16[4,2,3,48,768]{4,3,2,0,1:T(8,128)(2,1)}, u32[]{:S(2)}, u32[]{:S(2)}) collective-permute-start(bf16[4,2,3,48,768]{4,3,2,0,1:T(8,128)(2,1)S(1)} %copy.67), channel_id=1, source_target_pairs={{4,8},{8,4},{5,9},{9,5},{6,10},{10,6},{7,11},{11,7},{20,24},{24,20... | collective-permute-start | bytes 5308424 | tf_op jit(solution)/shard_map/ppermute | solution.py:636
  164.2 41.0 %collective-permute-start.8 = (bf16[4,2,3,48,768]{4,3,2,0,1:T(8,128)(2,1)S(1)}, bf16[4,2,3,48,768]{4,3,2,0,1:T(8,128)(2,1)}, u32[]{:S(2)}, u32[]{:S(2)}) collective-permute-start(bf16[4,2,3,48,768]{4,3,2,0,1:T(8,128)(2,1)S(1)} %copy.67), channel_id=1, source_target_pairs={{0,8},{4,0},{8,12},{12,4},{1,9},{5,1},{9,13},{13,5},{2,10},{6,2},{... | collective-permute-start | bytes 5308424 | tf_op jit(solution)/shard_map/ppermute | solution.py:635
  186.2 41.4 %all-to-all-start.3 = ((bf16[8,6,2,8224]{3,2,1,0:T(2,128)(2,1)}), bf16[8,6,2,8224]{3,2,1,0:T(2,128)(2,1)S(1)}, u32[]{:S(2)}, u32[]{:S(2)}) async-start(bf16[8,6,2,8224]{3,2,1,0:T(2,128)(2,1)} %pack.4), calls=%async_computation.3 | async-start | bytes 3194880 | tf_op jit(solution)/shard_map/all_to_all | solution.py:644
  227.6 1.2 copy-start.4
  228.7 47.7 %all-to-all-start.4 = ((bf16[8,6,2,8224]{3,2,1,0:T(2,128)(2,1)}), bf16[8,6,2,8224]{3,2,1,0:T(2,128)(2,1)S(1)}, u32[]{:S(2)}, u32[]{:S(2)}) async-start(bf16[8,6,2,8224]{3,2,1,0:T(2,128)(2,1)} %bitcast.82), calls=%async_computation.4 | async-start | bytes 3194880 | tf_op jit(solution)/shard_map/all_to_all | solution.py:652
  276.5 1.2 copy-start
  277.6 42.9 %all-to-all-start.5 = ((bf16[8,6,2,8224]{3,2,1,0:T(2,128)(2,1)}), bf16[8,6,2,8224]{3,2,1,0:T(2,128)(2,1)S(1)}, u32[]{:S(2)}, u32[]{:S(2)}) async-start(bf16[8,6,2,8224]{3,2,1,0:T(2,128)(2,1)} %bitcast.83), calls=%async_computation.5 | async-start | bytes 3194880 | tf_op jit(solution)/shard_map/all_to_all | solution.py:652
  320.5 1.2 copy-start.1
  320.5 4.8 %copy-start.5 = (f32[8224]{0:T(1024)S(1)}, f32[8224]{0:T(1024)}, u32[]{:S(2)}) copy-start(f32[8224]{0:T(1024)} %fusion.35) | copy-start | bytes 98692
  321.7 41.4 %all-to-all-start.6 = ((bf16[8,6,2,8224]{3,2,1,0:T(2,128)(2,1)}), bf16[8,6,2,8224]{3,2,1,0:T(2,128)(2,1)S(1)}, u32[]{:S(2)}, u32[]{:S(2)}) async-start(bf16[8,6,2,8224]{3,2,1,0:T(2,128)(2,1)} %bitcast.84), calls=%async_computation.6 | async-start | bytes 3194880 | tf_op jit(solution)/shard_map/all_to_all | solution.py:652
  363.1 1.2 copy-start.2
where the time goes:
time: 369 us; the launch traced here: 368 us
  Pallas kernels  200 us (54%)
  waiting for transfers between devices  69.1 us (19%)
  starting transfers between devices  44.5 us (12%)
  other arithmetic  29.4 us (8%)
  local copies, waits for them, and re-layouts  22.9 us (6%)
    pallas_call x3, Pallas kernels, grid_product(): pl.pallas_call(grid_kernel, grid=(fields // 6,), in_specs=[per_group] + [...  48.6 us
    pallas_call x3, Pallas kernels, synthesis(): pl.pallas_call(functools.partial(synthesis_kernel, slots=slots), grid_spe...  41.9 us
    pallas_call x3, Pallas kernels, analysis(): pl.pallas_call(functools.partial(analysis_kernel, slots=slots), grid_spec...  41.8 us
    pallas_call x1, Pallas kernels, legendre_table(): pl.pallas_call(functools.partial(table_kernel, lead=lead), grid=(pairs //...  40.3 us
    all_to_all x1, waiting for transfers between devices, shards_by_level(): lax.all_to_all(after(split, arrived, table), 'ma', split_axis=0, concat_a...  35.1 us
    all_to_all x3, waiting for transfers between devices, shards_by_level(): exchange(after(tendency.reshape(2 * count, TESTS * 3, 2, width), *last))  28.2 us
    pallas_call x3, Pallas kernels, pack_level(): pl.pallas_call(pack_kernel, grid=(targets,), in_specs=[pl.BlockSpec((piec...  16.3 us
    all_to_all x3, starting transfers between devices, shards_by_level(): exchange(after(tendency.reshape(2 * count, TESTS * 3, 2, width), *last))  12.2 us
  transfers between devices with their start and end apart: 16, of which 6 were waited for; matrix products, arithmetic and copies ran while one was open for 13% of the time, Pallas kernels for 53%

commit v1 on v0

--- a/solution.py
+++ b/solution.py
@@ -175,6 +175,7 @@
 VMEM_CAP = 56 << 20
 PAIR_ROWS = NM + 1
 CHUNK_ROWS = 16
+TABLE_PAIRS = 16
 SLOTS = 8
 
 
@@ -196,7 +197,7 @@
     return jnp.swapaxes(block, 0, 1)
 
 
-def table_kernel(upper, lower, first, second, seed_low, seed_high, cosine, out, *, lead):
+def table_kernel(upper, lower, first, second, seed_low, seed_high, cosine, _, out, *, lead):
     shape = seed_low.shape
     cosine_rows = jnp.broadcast_to(cosine[...], shape)
     first_step = first[...]
@@ -258,20 +259,7 @@
     lanes = lats.shape[0]
     spread_out = lambda values: jnp.broadcast_to(values[:, None], (pairs, lanes))
     chunks = window // CHUNK_ROWS
-    coefficient = pl.BlockSpec((chunks, 8, CHUNK_ROWS), lambda q: (0, q, 0))
-    per_pair = pl.BlockSpec((8, lanes), lambda q: (q, 0))
-    lead = -(-slots // CHUNK_ROWS)
-    return pl.pallas_call(
-        functools.partial(table_kernel, lead=lead),
-        grid=(pairs // 8,),
-        in_specs=[coefficient, coefficient, per_pair, per_pair, per_pair, per_pair]
-        + [pl.BlockSpec((1, lanes), lambda q: (0, 0))],
-        out_specs=pl.BlockSpec((8, window, lanes), lambda q: (q, 0, 0)),
-        out_shape=jax.ShapeDtypeStruct((pairs, window, lanes), BF16),
-        compiler_params=pltpu.CompilerParams(vmem_limit_bytes=VMEM_CAP),
-        cost_estimate=work(40),
-        name="table",
-    )(
+    operands = (
         by_chunk(upper),
         by_chunk(lower),
         spread_out(slot),
@@ -280,6 +268,34 @@
         seed_high,
         jnp.cos(colatitude)[None, :],
     )
+    blocks = pairs // TABLE_PAIRS
+    shape = jax.ShapeDtypeStruct((pairs, window, lanes), BF16)
+    halves = []
+    for begin, end in ((0, blocks // 2), (blocks // 2, blocks)):
+        place = lambda q, begin=begin: q + begin
+        coefficient = pl.BlockSpec(
+            (chunks, TABLE_PAIRS, CHUNK_ROWS), lambda q, place=place: (0, place(q), 0)
+        )
+        per_pair = pl.BlockSpec((TABLE_PAIRS, lanes), lambda q, place=place: (place(q), 0))
+        before = halves[-1:] or [jnp.zeros((8, 128), BF16)]
+        halves.append(
+            pl.pallas_call(
+                functools.partial(table_kernel, lead=-(-slots // CHUNK_ROWS)),
+                grid=(end - begin,),
+                in_specs=[coefficient, coefficient, per_pair, per_pair, per_pair, per_pair]
+                + [pl.BlockSpec((1, lanes), lambda q: (0, 0))]
+                + [pl.BlockSpec(memory_space=pl.ANY)],
+                out_specs=pl.BlockSpec(
+                    (TABLE_PAIRS, window, lanes), lambda q, place=place: (place(q), 0, 0)
+                ),
+                out_shape=shape,
+                input_output_aliases={7: 0} if halves else {},
+                compiler_params=pltpu.CompilerParams(vmem_limit_bytes=VMEM_CAP),
+                cost_estimate=work(20),
+                name="table",
+            )(*operands, *before)
+        )
+    return halves
 
 
 def row_mask(switch, source, place, slots, lane):
@@ -570,11 +586,12 @@
     width = section.shape[-1]
     depth = LEV // (2 * count)
     band = velocity.shape[0]
-    half = band // 2
     place = lax.axis_index("ma")
     across = lax.axis_index("x")
     core = lax.axis_index("k")
     swap_cores = [(0, 1), (1, 0)]
+    by_level = section.reshape(TESTS * 3, 2 * count, depth, 2, width)
+    sent = pack_level(by_level, 0)
     every_pair = gather_pairs(pair_list, count)
     slot_of = jnp.arange(count * slots, dtype=jnp.int32) % slots
     switch = slot_of + NM - every_pair
@@ -586,28 +603,37 @@
     forcing = lax.dynamic_slice_in_dim(forcing, (core * count + place) * depth, depth, axis=1)
     forcing = jnp.stack([forcing, jnp.zeros_like(forcing)], axis=1).reshape(-1, depth)
 
-    by_level = section.reshape(TESTS * 3, 2 * count, depth, 2, width)
     exchange = functools.partial(
         lax.all_to_all, axis_name=("k", "ma"), split_axis=0, concat_axis=0, tiled=True
     )
-    sent = pack_level(by_level, 0)
     arrived = exchange(sent)
     specs = [arrived]
 
-    bands = after(velocity, sent).reshape(2, half, 3, LEV // 4, NLON).transpose(0, 3, 2, 1, 4)
-    mine = lax.dynamic_index_in_dim(bands, core, 0, keepdims=False)
-    theirs = lax.dynamic_index_in_dim(bands, 1 - core, 0, keepdims=False)
-    theirs = lax.ppermute(theirs, "k", swap_cores)
-    split = jnp.where(core == 0, jnp.stack([mine, theirs]), jnp.stack([theirs, mine]))
-    split = split.reshape(count, depth, 3, half, NLON)
+    side = count // 2
+    bands = velocity.transpose(2, 1, 0, 3)
+    pieces = []
+    for turn in range(side):
+        block = lax.dynamic_slice_in_dim(bands, (place + turn) % side * depth, depth, axis=0)
+        route = [
+            (
+                sender * count + origin,
+                origin // side * count + sender * side + (origin + turn) % side,
+            )
+            for sender in range(2)
+            for origin in range(count)
+        ]
+        pieces.append(lax.ppermute(block, ("k", "ma"), route))
 
     mid = NLAT // 2
     north = jnp.arange(mid, dtype=jnp.int32)
     lats = jnp.concatenate(
         [north[:128], NLAT - 1 - north[:128], north[128:], NLAT - 1 - north[128:]]
     )
-    arrange = (jnp.arange(NLAT, dtype=jnp.int32)[:, None] == lats[None, :]).astype(BF16)
-    table = legendre_table(every_pair, slots, jnp.concatenate([north, north[128:]]))
+    shift = (place - jnp.arange(side, dtype=jnp.int32)) % side
+    origin = side * jnp.stack([1 - across, across])[None, :] + shift[:, None]
+    rows = band * origin[:, :, None] + jnp.arange(band, dtype=jnp.int32)
+    arrange = (rows.reshape(-1)[:, None] == lats[None, :]).astype(BF16)
+    half_table, table = legendre_table(every_pair, slots, jnp.concatenate([north, north[128:]]))
     order_list = jnp.stack([every_pair, NM - 1 - every_pair], axis=1).reshape(-1)
     waves = wave_table(order_list, NLON)
     inverse_table = (waves * grid_scale).astype(BF16)
@@ -622,31 +648,30 @@
     total = start[0] - (step_weight * diffusion) * spread * section[0].astype(F32)
     total = total.reshape(TESTS, 3, 2, count, depth, 2, width)
 
-    own_first = (across == 0) & (core == 0)
-    own_second = (across == 1) & (core == 1)
-
-    held = lax.all_to_all(
-        after(split, arrived, table), "ma", split_axis=0, concat_axis=0, tiled=True
-    )
     winds = []
-    last = ()
+    last = (arrived,)
     for group in (slice(0, 1), slice(1, depth)):
-        part = after(held[:, group], *last)
+        part = after(jnp.stack([piece[group] for piece in pieces], axis=1), *last)
         turn = lax.ppermute(part, ("x", "k"), [(0, 2), (1, 0), (2, 3), (3, 1)])
         cross = lax.ppermute(part, ("x", "k"), [(1, 2), (2, 1)])
-        first = jnp.where(own_first, part, jnp.where((across == 0) & (core == 1), cross, turn))
-        second = jnp.where(own_second, part, jnp.where((across == 1) & (core == 0), cross, turn))
-        winds += [(first[:, k], second[:, k]) for k in range(first.shape[1])]
+        other = jnp.where(across == core, part, cross)
+        winds += [(turn[k], other[k]) for k in range(turn.shape[0])]
         last = (turn, cross)
 
-    last = (held,)
+    first_spectra = synthesis(
+        arrived.reshape(2, count, TESTS * 3, 2, width), table, forcing[:, :1], switch, slots
+    )
+    last = (arrived,)
     for level in range(1, depth):
-        specs.append(exchange(after(pack_level(by_level, level), *last)))
+        packed = pack_level(by_level if level == 1 else after(by_level, arrived), level)
+        specs.append(exchange(after(packed, *last)))
         last = (specs[-1],)
     specs = [spec.reshape(2, count, TESTS * 3, 2, width) for spec in specs]
 
     for level in range(depth):
-        spectra = synthesis(specs[level], table, forcing[:, level : level + 1], switch, slots)
+        spectra = first_spectra
+        if level:
+            spectra = synthesis(specs[level], table, forcing[:, level : level + 1], switch, slots)
         fourier = grid_product(spectra, *winds[level], arrange, tables, weights)
         tendency = analysis(fourier, table, switch, slots, width)
         back = exchange(after(tendency.reshape(2 * count, TESTS * 3, 2, width), *last))
@@ -659,7 +684,7 @@
     sizes = dict(mesh.shape)
     count = sizes["ma"]
     whole_slots = (NM // 2) % (count * SLOTS) == 0
-    if sizes["team"] == 4 and LEV % (2 * count) == 0 and whole_slots:
+    if sizes["team"] == 4 and count % 2 == 0 and LEV % (2 * count) == 0 and whole_slots:
         grid = Mesh(
             mesh.devices.reshape(sizes["run"], 2, 2, count), ("run", "x", "k", "ma")
         )

time: 369 us -> 340 us (0.921)
  waiting for transfers between devices: 69.1 us -> 33.8 us
  starting transfers between devices: 44.5 us -> 61.8 us
  Pallas kernels: 200 us -> 191 us
  other arithmetic: 29.4 us -> 24.2 us
    all_to_all x3 -> x2, waiting for transfers between devices: 38.7 us -> 5.62 us  [shards_by_level(): specs.append(exchange(after(packed, *last)))]
    ppermute x1 -> x2, starting transfers between devices: 0.41 us -> 12.3 us  [shards_by_level(): pieces.append(lax.ppermute(block, ('k', 'ma'), route))]
    pallas_call x1 -> x2, Pallas kernels: 40.3 us -> 31.2 us  [legendre_table(): pl.pallas_call(functools.partial(table_kernel, lead=-(-slots // CHUNK_ROW...]
    all_to_all x3 -> x2, starting transfers between devices: 12.9 us -> 18.5 us  [shards_by_level(): specs.append(exchange(after(packed, *last)))]
    another operation x0 -> x5, local copies, waits for them, and re-layouts: none -> 4.25 us  [the longest x4 2.36 us: shards_by_level(): part = after(jnp.stack([piece[group] for piece in pieces], axis=1), *last)]
    select_n x2, other arithmetic: 4.23 us -> 0.26 us  [the longest x1 0.19 us: shards_by_level(): other = jnp.where(across == core, part, cross)]
    unnamed x16 -> x19, local copies, waits for them, and re-layouts: 6.03 us -> 9.5 us
  transfers between devices with their start and end apart: 16 -> 16, of which waited for: 6 -> 3; matrix products, arithmetic and copies ran while one was open for 13% -> 12% of each run, Pallas kernels for 53% -> 55%
where the time goes in v1:
time: 340 us; the launch traced here: 338 us
  Pallas kernels  191 us (56%)
  starting transfers between devices  61.8 us (18%)
  waiting for transfers between devices  33.8 us (10%)
  local copies, waits for them, and re-layouts  25.1 us (7%)
  other arithmetic  24.2 us (7%)
    pallas_call x3, Pallas kernels, grid_product(): pl.pallas_call(grid_kernel, grid=(fields // 6,), in_specs=[per_group] + [...  48.5 us
    pallas_call x3, Pallas kernels, synthesis(): pl.pallas_call(functools.partial(synthesis_kernel, slots=slots), grid_spe...  41.9 us
    pallas_call x3, Pallas kernels, analysis(): pl.pallas_call(functools.partial(analysis_kernel, slots=slots), grid_spec...  41.8 us
    pallas_call x2, Pallas kernels, legendre_table(): pl.pallas_call(functools.partial(table_kernel, lead=-(-slots // CHUNK_ROW...  31.2 us
    all_to_all x3, waiting for transfers between devices, shards_by_level(): exchange(after(tendency.reshape(2 * count, TESTS * 3, 2, width), *last))  28.2 us
    all_to_all x2, starting transfers between devices, shards_by_level(): specs.append(exchange(after(packed, *last)))  18.5 us
    pallas_call x3, Pallas kernels, pack_level(): pl.pallas_call(pack_kernel, grid=(targets,), in_specs=[pl.BlockSpec((piec...  16.3 us
    ppermute x2, starting transfers between devices, shards_by_level(): pieces.append(lax.ppermute(block, ('k', 'ma'), route))  12.3 us
  transfers between devices with their start and end apart: 16, of which 3 were waited for; matrix products, arithmetic and copies ran while one was open for 12% of the time, Pallas kernels for 55%

profile of v1, /device:TPU:0, one launch (start us, length us, event | category | flops | bytes accessed | tf_op | source)
XLA Modules:
  0.0 337.9 jit_solution(4051794728964062554)
XLA Ops:
  10.8 5.4 %pack.3 = bf16[8,6,2,8224]{3,2,1,0:T(2,128)(2,1)} custom-call(bf16[6,8,3,2,8224]{4,3,2,1,0:T(2,128)(2,1)} %bitcast.78), custom_call_target="tpu_custom_call" | custom-call | flops 5000000000 | bytes 5000000 | tf_op jit(solution)/shard_map/pack/pallas_call | solution.py:533
  16.2 4.3 %all-to-all-start = ((bf16[8,6,2,8224]{3,2,1,0:T(2,128)(2,1)}), bf16[8,6,2,8224]{3,2,1,0:T(2,128)(2,1)}, u32[]{:S(2)}, u32[]{:S(2)}) async-start(bf16[8,6,2,8224]{3,2,1,0:T(2,128)(2,1)} %pack.3), calls=%async_computation | async-start | bytes 3194880 | tf_op jit(solution)/shard_map/all_to_all | solution.py:609
  21.6 5.4 %pack.5 = bf16[8,6,2,8224]{3,2,1,0:T(2,128)(2,1)} custom-call(bf16[6,8,3,2,8224]{4,3,2,1,0:T(2,128)(2,1)} %bitcast.79), custom_call_target="tpu_custom_call" | custom-call | flops 5000000000 | bytes 5000000 | tf_op jit(solution)/shard_map/pack/pallas_call | solution.py:533
  31.9 11.7 %collective-permute-start.4 = (bf16[3,3,96,768]{3,2,1,0:T(8,128)(2,1)}, bf16[3,3,96,768]{3,2,1,0:T(8,128)(2,1)}, u32[]{:S(2)}, u32[]{:S(2)}) collective-permute-start(bf16[3,3,96,768]{3,2,1,0:T(8,128)(2,1)} %bitcast.86), channel_id=1, source_target_pairs={{0,0},{1,1},{2,4},{3,5},{4,2},{5,3},{6,6},{7,7},{8,8},{9,9},{10,12... | collective-permute-start | bytes 3981320 | tf_op jit(solution)/shard_map/ppermute | solution.py:625
  61.2 15.6 %table.2._ = bf16[128,288,256]{2,1,0:T(8,128)(2,1)} custom-call(f32[18,128,16]{2,1,0:T(8,128)} %get-tuple-element.36.upper, f32[18,128,16]{2,1,0:T(8,128)} %get-tuple-element.35.lower, s32[128,256]{1,0:T(8,128)} %broadcast_in_dim.69.first, s32[128,256]{1,0:T(8,128)} %broadcast_in_dim.70.second, f32[128,256]{1,0:T(8,128)} %get-tuple-element.55.seed_low, ...), custom_call_target="tpu_custom_call" | custom-call | flops 20000000000 | bytes 20000000 | tf_op jit(solution)/shard_map/table/pallas_call | solution.py:282
  76.8 15.6 %table.3 = bf16[128,288,256]{2,1,0:T(8,128)(2,1)} custom-call(f32[18,128,16]{2,1,0:T(8,128)} %get-tuple-element.36.upper, f32[18,128,16]{2,1,0:T(8,128)} %get-tuple-element.35.lower, s32[128,256]{1,0:T(8,128)} %broadcast_in_dim.69.first, s32[128,256]{1,0:T(8,128)} %broadcast_in_dim.70.second, ...), custom_call_target="tpu_custom_call", output_to_operand_aliasing={{}: (7, {})} | custom-call | flops 20000000000 | bytes 20000000 | tf_op jit(solution)/shard_map/table/pallas_call | solution.py:282
  99.6 14.4 %all-to-all-start.1 = ((bf16[8,6,2,8224]{3,2,1,0:T(2,128)(2,1)}), bf16[8,6,2,8224]{3,2,1,0:T(2,128)(2,1)}, u32[]{:S(2)}, u32[]{:S(2)}) async-start(bf16[8,6,2,8224]{3,2,1,0:T(2,128)(2,1)} %pack.5), calls=%async_computation.1 | async-start | bytes 3194880 | tf_op jit(solution)/shard_map/all_to_all | solution.py:667
  114.0 14.0 %synthesis.3.spectra = bf16[24,256,384]{2,1,0:T(8,128)(2,1)} custom-call(s32[128]{0:T(128)} %get-tuple-element.62.switch, bf16[2,4,6,2,8224]{4,3,2,1,0:T(2,128)(2,1)} %bitcast.7.spec, bf16[128,288,256]{2,1,0:T(8,128)(2,1)} %table.3, f32[24,1]{1,0:T(8,128)} %get-tuple-element.39.forcing), custom_call_target="tpu_custom_call" | custom-call | flops 14000000000 | bytes 14000000 | tf_op jit(solution)/shard_map/synthesis/pallas_call | solution.py:374
  128.0 5.4 %pack.4 = bf16[8,6,2,8224]{3,2,1,0:T(2,128)(2,1)} custom-call(bf16[6,8,3,2,8224]{4,3,2,1,0:T(2,128)(2,1)} %bitcast.80), custom_call_target="tpu_custom_call" | custom-call | flops 5000000000 | bytes 5000000 | tf_op jit(solution)/shard_map/pack/pallas_call | solution.py:533
  139.5 16.2 %grid_product.3.fourier = bf16[24,256,384]{2,1,0:T(8,128)(2,1)} custom-call(bf16[24,256,384]{2,1,0:T(8,128)(2,1)} %synthesis.3.spectra, bf16[2,3,96,768]{3,2,1,0:T(8,128)(2,1)} %bitcast.19.first, bf16[2,3,96,768]{3,2,1,0:T(8,128)(2,1)} %select_bitcast_fusion.second, bf16[384,384]{1,0:T(8,128)(2,1)} %compare_convert_fusion.arrange, ...), custom_call_target="tpu_custom_call" | custom-call | flops 16000000000 | bytes 16000000 | tf_op jit(solution)/shard_map/grid_product/pallas_call | solution.py:438
  155.6 4.0 %all-to-all-start.2 = ((bf16[8,6,2,8224]{3,2,1,0:T(2,128)(2,1)}), bf16[8,6,2,8224]{3,2,1,0:T(2,128)(2,1)S(1)}, u32[]{:S(2)}, u32[]{:S(2)}) async-start(bf16[8,6,2,8224]{3,2,1,0:T(2,128)(2,1)} %pack.4), calls=%async_computation.2 | async-start | bytes 3194880 | tf_op jit(solution)/shard_map/all_to_all | solution.py:667
  159.6 14.0 %analysis.3 = bf16[2,4,6,2,8224]{4,3,2,1,0:T(2,128)(2,1)} custom-call(s32[128]{0:T(128)} %get-tuple-element.62.switch, bf16[24,256,384]{2,1,0:T(8,128)(2,1)} %grid_product.3.fourier, bf16[128,288,256]{2,1,0:T(8,128)(2,1)} %table.3), custom_call_target="tpu_custom_call" | custom-call | flops 14000000000 | bytes 14000000 | tf_op jit(solution)/shard_map/analysis/pallas_call | solution.py:509
  177.9 14.0 %synthesis.4.spectra = bf16[24,256,384]{2,1,0:T(8,128)(2,1)} custom-call(s32[128]{0:T(128)} %get-tuple-element.62.switch, bf16[2,4,6,2,8224]{4,3,2,1,0:T(2,128)(2,1)} %bitcast.34.spec, bf16[128,288,256]{2,1,0:T(8,128)(2,1)} %table.3, f32[24,1]{1,0:T(8,128)} %get-tuple-element.38.forcing), custom_call_target="tpu_custom_call" | custom-call | flops 14000000000 | bytes 14000000 | tf_op jit(solution)/shard_map/synthesis/pallas_call | solution.py:374
  191.9 5.6 %all-to-all-done.2 = bf16[8,6,2,8224]{3,2,1,0:T(2,128)(2,1)S(1)} async-done(((bf16[8,6,2,8224]{3,2,1,0:T(2,128)(2,1)}), bf16[8,6,2,8224]{3,2,1,0:T(2,128)(2,1)S(1)}, u32[]{:S(2)}, u32[]{:S(2)}) %all-to-all-start.2) | async-done | bytes 1579040 | tf_op jit(solution)/shard_map/all_to_all | solution.py:667
  202.3 16.2 %grid_product.4.fourier = bf16[24,256,384]{2,1,0:T(8,128)(2,1)} custom-call(bf16[24,256,384]{2,1,0:T(8,128)(2,1)} %synthesis.4.spectra, bf16[2,3,96,768]{3,2,1,0:T(8,128)(2,1)} %get-tuple-element.28.first, bf16[2,3,96,768]{3,2,1,0:T(8,128)(2,1)} %get-tuple-element.26.second, bf16[384,384]{1,0:T(8,128)(2,1)} %compare_convert_fusion.arrange, ...), custom_call_target="tpu_custom_call" | custom-call | flops 16000000000 | bytes 16000000 | tf_op jit(solution)/shard_map/grid_product/pallas_call | solution.py:438
  218.5 13.9 %analysis.4 = bf16[2,4,6,2,8224]{4,3,2,1,0:T(2,128)(2,1)} custom-call(s32[128]{0:T(128)} %get-tuple-element.62.switch, bf16[24,256,384]{2,1,0:T(8,128)(2,1)} %grid_product.4.fourier, bf16[128,288,256]{2,1,0:T(8,128)(2,1)} %table.3), custom_call_target="tpu_custom_call" | custom-call | flops 14000000000 | bytes 14000000 | tf_op jit(solution)/shard_map/analysis/pallas_call | solution.py:509
  232.4 14.0 %synthesis.5.spectra = bf16[24,256,384]{2,1,0:T(8,128)(2,1)} custom-call(s32[128]{0:T(128)} %get-tuple-element.62.switch, bf16[2,4,6,2,8224]{4,3,2,1,0:T(2,128)(2,1)} %bitcast.82, bf16[128,288,256]{2,1,0:T(8,128)(2,1)} %table.3, f32[24,1]{1,0:T(8,128)} %get-tuple-element.37.forcing), custom_call_target="tpu_custom_call" | custom-call | flops 14000000000 | bytes 14000000 | tf_op jit(solution)/shard_map/synthesis/pallas_call | solution.py:374
  247.6 5.0 %all-to-all-start.4 = ((bf16[8,6,2,8224]{3,2,1,0:T(2,128)(2,1)}), bf16[8,6,2,8224]{3,2,1,0:T(2,128)(2,1)S(1)}, u32[]{:S(2)}, u32[]{:S(2)}) async-start(bf16[8,6,2,8224]{3,2,1,0:T(2,128)(2,1)} %bitcast.84), calls=%async_computation.4 | async-start | bytes 3194880 | tf_op jit(solution)/shard_map/all_to_all | solution.py:677
  252.6 16.2 %grid_product.5.fourier = bf16[24,256,384]{2,1,0:T(8,128)(2,1)} custom-call(bf16[24,256,384]{2,1,0:T(8,128)(2,1)} %synthesis.5.spectra, bf16[2,3,96,768]{3,2,1,0:T(8,128)(2,1)} %get-tuple-element.27.first, bf16[2,3,96,768]{3,2,1,0:T(8,128)(2,1)} %get-tuple-element.25.second, bf16[384,384]{1,0:T(8,128)(2,1)} %compare_convert_fusion.arrange, ...), custom_call_target="tpu_custom_call" | custom-call | flops 16000000000 | bytes 16000000 | tf_op jit(solution)/shard_map/grid_product/pallas_call | solution.py:438
  268.8 14.0 %analysis.5 = bf16[2,4,6,2,8224]{4,3,2,1,0:T(2,128)(2,1)} custom-call(s32[128]{0:T(128)} %get-tuple-element.62.switch, bf16[24,256,384]{2,1,0:T(8,128)(2,1)} %grid_product.5.fourier, bf16[128,288,256]{2,1,0:T(8,128)(2,1)} %table.3), custom_call_target="tpu_custom_call" | custom-call | flops 14000000000 | bytes 14000000 | tf_op jit(solution)/shard_map/analysis/pallas_call | solution.py:509
  282.8 7.8 %all-to-all-done.4 = bf16[8,6,2,8224]{3,2,1,0:T(2,128)(2,1)S(1)} async-done(((bf16[8,6,2,8224]{3,2,1,0:T(2,128)(2,1)}), bf16[8,6,2,8224]{3,2,1,0:T(2,128)(2,1)S(1)}, u32[]{:S(2)}, u32[]{:S(2)}) %all-to-all-start.4) | async-done | bytes 1579040 | tf_op jit(solution)/shard_map/all_to_all | solution.py:677
  295.3 10.1 %fusion.base = f32[2,3,2,4,3,2,8224]{6,5,4,3,2,1,0:T(2,128)} fusion(f32[2,3,2,4,3,2,8224]{6,5,4,3,2,1,0:T(2,128)} %bitcast.74, bf16[2,3,2,4,3,2,8224]{6,5,4,3,2,1,0:T(2,128)(2,1)} %bitcast.81, f32[8224]{0:T(1024)S(1)} %copy-done.6), kind=kLoop, calls=%fused_computation.1 | loop fusion | flops 7105536 | bytes 23718016 | tf_op jit(solution)/shard_map/sub | solution.py:648
  305.3 3.7 %finish.3.base = f32[2,3,2,4,3,2,8224]{6,5,4,3,2,1,0:T(2,128)} custom-call(f32[2,3,2,4,3,2,8224]{6,5,4,3,2,1,0:T(2,128)} %fusion.base, bf16[2,4,6,2,8224]{4,3,2,1,0:T(2,128)(2,1)} %bitcast.75), custom_call_target="tpu_custom_call", output_to_operand_aliasing={{}: (0, {})} | custom-call | flops 5000000000 | bytes 5000000 | tf_op jit(solution)/shard_map/finish/pallas_call | solution.py:557
  312.6 20.4 %all-to-all-done.5 = bf16[8,6,2,8224]{3,2,1,0:T(2,128)(2,1)S(1)} async-done(((bf16[8,6,2,8224]{3,2,1,0:T(2,128)(2,1)}), bf16[8,6,2,8224]{3,2,1,0:T(2,128)(2,1)S(1)}, u32[]{:S(2)}, u32[]{:S(2)}) %all-to-all-start.5) | async-done | bytes 1579040 | tf_op jit(solution)/shard_map/all_to_all | solution.py:677
  (115 shorter events, 68.9 us)
Async XLA Ops:
  0.0 47.2 %collective-permute-start = (s32[32]{0:T(128)}, s32[32]{0:T(128)S(1)}, u32[]{:S(2)}, u32[]{:S(2)}) collective-permute-start(s32[32]{0:T(128)} %param.8), channel_id=1, source_target_pairs={{0,1},{1,2},{2,3},{3,0},{4,5},{5,6},{6,7},{7,4},{8,9},{9,10},{10,1... | collective-permute-start | bytes 392 | tf_op jit(solution)/shard_map/ppermute | solution.py:579
  3.0 44.2 %collective-permute-start.1 = (s32[32]{0:T(128)}, s32[32]{0:T(128)S(1)}, u32[]{:S(2)}, u32[]{:S(2)}) collective-permute-start(s32[32]{0:T(128)} %param.8), channel_id=1, source_target_pairs={{0,2},{1,3},{2,0},{3,1},{4,6},{5,7},{6,4},{7,5},{8,10},{9,11},{10,... | collective-permute-start | bytes 392 | tf_op jit(solution)/shard_map/ppermute | solution.py:579
  5.6 41.7 %collective-permute-start.2 = (s32[32]{0:T(128)}, s32[32]{0:T(128)S(1)}, u32[]{:S(2)}, u32[]{:S(2)}) collective-permute-start(s32[32]{0:T(128)} %param.8), channel_id=1, source_target_pairs={{0,3},{1,0},{2,1},{3,2},{4,7},{5,4},{6,5},{7,6},{8,11},{9,8},{10,9... | collective-permute-start | bytes 392 | tf_op jit(solution)/shard_map/ppermute | solution.py:579
  10.1 82.3 %collective-permute-start.5 = (bf16[3,3,96,768]{3,2,1,0:T(8,128)(2,1)}, bf16[3,3,96,768]{3,2,1,0:T(8,128)(2,1)S(1)}, u32[]{:S(2)}, u32[]{:S(2)}) collective-permute-start(bf16[3,3,96,768]{3,2,1,0:T(8,128)(2,1)} %bitcast.71), channel_id=1, source_target_pairs={{0,1},{1,0},{2,5},{3,4},{4,3},{5,2},{6,7},{7,6},{8,9},{9,8},{10,13... | collective-permute-start | bytes 3981320 | tf_op jit(solution)/shard_map/ppermute | solution.py:625
  16.2 81.2 %all-to-all-start = ((bf16[8,6,2,8224]{3,2,1,0:T(2,128)(2,1)}), bf16[8,6,2,8224]{3,2,1,0:T(2,128)(2,1)}, u32[]{:S(2)}, u32[]{:S(2)}) async-start(bf16[8,6,2,8224]{3,2,1,0:T(2,128)(2,1)} %pack.3), calls=%async_computation | async-start | bytes 3194880 | tf_op jit(solution)/shard_map/all_to_all | solution.py:609
  20.5 11.3 %collective-permute-start.3 = (s32[1]{0:T(128)}, s32[1]{0:T(128)}, u32[]{:S(2)}, u32[]{:S(2)}) collective-permute-start(s32[1]{0:T(128)} %param.9), channel_id=1, source_target_pairs={{0,4},{4,0},{1,5},{5,1},{2,6},{6,2},{3,7},{7,3},{8,12},{12,8},{9,1... | collective-permute-start | bytes 20 | tf_op jit(solution)/shard_map/ppermute | solution.py:599
  21.6 5.5 %copy-start.7 = (s32[32]{0:T(128)S(1)}, s32[32]{0:T(128)}, u32[]{:S(2)}) copy-start(s32[32]{0:T(128)} %param.8) | copy-start | bytes 388
  31.9 60.6 %collective-permute-start.4 = (bf16[3,3,96,768]{3,2,1,0:T(8,128)(2,1)}, bf16[3,3,96,768]{3,2,1,0:T(8,128)(2,1)}, u32[]{:S(2)}, u32[]{:S(2)}) collective-permute-start(bf16[3,3,96,768]{3,2,1,0:T(8,128)(2,1)} %bitcast.86), channel_id=1, source_target_pairs={{0,0},{1,1},{2,4},{3,5},{4,2},{5,3},{6,6},{7,7},{8,8},{9,9},{10,12... | collective-permute-start | bytes 3981320 | tf_op jit(solution)/shard_map/ppermute | solution.py:625
  92.4 1.1 copy-start.4
  94.6 1.3 copy-start.5
  97.4 36.1 %collective-permute-start.6 = (bf16[1,2,3,96,768]{4,3,2,1,0:T(8,128)(2,1)S(1)}, bf16[1,2,3,96,768]{4,3,2,1,0:T(8,128)(2,1)}, u32[]{:S(2)}, u32[]{:S(2)}) collective-permute-start(bf16[1,2,3,96,768]{4,3,2,1,0:T(8,128)(2,1)S(1)} %pad_maximum_fusion.2), channel_id=1, source_target_pairs={{0,8},{4,0},{8,12},{12,4},{1,9},{5,1},{9,13},{13,5},{2,10},{6,2},{... | collective-permute-start | bytes 2654216 | tf_op jit(solution)/shard_map/ppermute | solution.py:655
  98.9 34.6 %collective-permute-start.7 = (bf16[1,2,3,96,768]{4,3,2,1,0:T(8,128)(2,1)S(1)}, bf16[1,2,3,96,768]{4,3,2,1,0:T(8,128)(2,1)S(1)}, u32[]{:S(2)}, u32[]{:S(2)}) collective-permute-start(bf16[1,2,3,96,768]{4,3,2,1,0:T(8,128)(2,1)S(1)} %pad_maximum_fusion.2), channel_id=1, source_target_pairs={{4,8},{8,4},{5,9},{9,5},{6,10},{10,6},{7,11},{11,7},{20,24},{24,20... | collective-permute-start | bytes 2654216 | tf_op jit(solution)/shard_map/ppermute | solution.py:656
  99.6 56.0 %all-to-all-start.1 = ((bf16[8,6,2,8224]{3,2,1,0:T(2,128)(2,1)}), bf16[8,6,2,8224]{3,2,1,0:T(2,128)(2,1)}, u32[]{:S(2)}, u32[]{:S(2)}) async-start(bf16[8,6,2,8224]{3,2,1,0:T(2,128)(2,1)} %pack.5), calls=%async_computation.1 | async-start | bytes 3194880 | tf_op jit(solution)/shard_map/all_to_all | solution.py:667
  133.5 40.1 %collective-permute-start.9 = (bf16[2,2,3,96,768]{4,3,2,1,0:T(8,128)(2,1)S(1)}, bf16[2,2,3,96,768]{4,3,2,1,0:T(8,128)(2,1)}, u32[]{:S(2)}, u32[]{:S(2)}) collective-permute-start(bf16[2,2,3,96,768]{4,3,2,1,0:T(8,128)(2,1)S(1)} %pad_maximum_fusion), channel_id=1, source_target_pairs={{4,8},{8,4},{5,9},{9,5},{6,10},{10,6},{7,11},{11,7},{20,24},{24,20... | collective-permute-start | bytes 5308424 | tf_op jit(solution)/shard_map/ppermute | solution.py:656
  135.3 39.8 %collective-permute-start.8 = (bf16[2,2,3,96,768]{4,3,2,1,0:T(8,128)(2,1)S(1)}, bf16[2,2,3,96,768]{4,3,2,1,0:T(8,128)(2,1)}, u32[]{:S(2)}, u32[]{:S(2)}) collective-permute-start(bf16[2,2,3,96,768]{4,3,2,1,0:T(8,128)(2,1)S(1)} %pad_maximum_fusion), channel_id=1, source_target_pairs={{0,8},{4,0},{8,12},{12,4},{1,9},{5,1},{9,13},{13,5},{2,10},{6,2},{... | collective-permute-start | bytes 5308424 | tf_op jit(solution)/shard_map/ppermute | solution.py:655
  155.6 41.9 %all-to-all-start.2 = ((bf16[8,6,2,8224]{3,2,1,0:T(2,128)(2,1)}), bf16[8,6,2,8224]{3,2,1,0:T(2,128)(2,1)S(1)}, u32[]{:S(2)}, u32[]{:S(2)}) async-start(bf16[8,6,2,8224]{3,2,1,0:T(2,128)(2,1)} %pack.4), calls=%async_computation.2 | async-start | bytes 3194880 | tf_op jit(solution)/shard_map/all_to_all | solution.py:667
  197.5 1.2 copy-start.3
  198.7 47.7 %all-to-all-start.3 = ((bf16[8,6,2,8224]{3,2,1,0:T(2,128)(2,1)}), bf16[8,6,2,8224]{3,2,1,0:T(2,128)(2,1)S(1)}, u32[]{:S(2)}, u32[]{:S(2)}) async-start(bf16[8,6,2,8224]{3,2,1,0:T(2,128)(2,1)} %bitcast.83), calls=%async_computation.3 | async-start | bytes 3194880 | tf_op jit(solution)/shard_map/all_to_all | solution.py:677
  246.4 1.2 copy-start
  247.6 42.9 %all-to-all-start.4 = ((bf16[8,6,2,8224]{3,2,1,0:T(2,128)(2,1)}), bf16[8,6,2,8224]{3,2,1,0:T(2,128)(2,1)S(1)}, u32[]{:S(2)}, u32[]{:S(2)}) async-start(bf16[8,6,2,8224]{3,2,1,0:T(2,128)(2,1)} %bitcast.84), calls=%async_computation.4 | async-start | bytes 3194880 | tf_op jit(solution)/shard_map/all_to_all | solution.py:677
  290.5 1.2 copy-start.1
  290.5 4.7 %copy-start.6 = (f32[8224]{0:T(1024)S(1)}, f32[8224]{0:T(1024)}, u32[]{:S(2)}) copy-start(f32[8224]{0:T(1024)} %fusion.34) | copy-start | bytes 98692
  291.7 41.4 %all-to-all-start.5 = ((bf16[8,6,2,8224]{3,2,1,0:T(2,128)(2,1)}), bf16[8,6,2,8224]{3,2,1,0:T(2,128)(2,1)S(1)}, u32[]{:S(2)}, u32[]{:S(2)}) async-start(bf16[8,6,2,8224]{3,2,1,0:T(2,128)(2,1)} %bitcast.85), calls=%async_computation.5 | async-start | bytes 3194880 | tf_op jit(solution)/shard_map/all_to_all | solution.py:677
  333.1 1.2 copy-start.2

commit v2 on v1

--- a/solution.py
+++ b/solution.py
@@ -176,7 +176,7 @@
 PAIR_ROWS = NM + 1
 CHUNK_ROWS = 16
 TABLE_PAIRS = 16
-SLOTS = 8
+SLOTS = 16
 
 
 def work(micros):
@@ -390,7 +390,7 @@
     )(switch, spec, table, forcing)
 
 
-LON_TILE = 256
+LON_TILE = 768
 
 
 def grid_kernel(
@@ -663,7 +663,7 @@
     )
     last = (arrived,)
     for level in range(1, depth):
-        packed = pack_level(by_level if level == 1 else after(by_level, arrived), level)
+        packed = pack_level(by_level, level)
         specs.append(exchange(after(packed, *last)))
         last = (specs[-1],)
     specs = [spec.reshape(2, count, TESTS * 3, 2, width) for spec in specs]

time: 340 us -> 335 us (0.985)
  starting transfers between devices: 61.8 us -> 56.8 us
  Pallas kernels: 191 us -> 187 us
  waiting for transfers between devices: 33.8 us -> 37.2 us
    all_to_all x2, starting transfers between devices: 18.5 us -> 12.9 us  [shards_by_level(): specs.append(exchange(after(packed, *last)))]
  transfers between devices with their start and end apart: 16 -> 16, of which waited for: 3 -> 4; matrix products, arithmetic and copies ran while one was open for 12% -> 13% of each run, Pallas kernels for 55% -> 55%
where the time goes in v2:
time: 335 us; the launch traced here: 333 us
  Pallas kernels  187 us (56%)
  starting transfers between devices  56.8 us (17%)
  waiting for transfers between devices  37.2 us (11%)
  local copies, waits for them, and re-layouts  25 us (7%)
  other arithmetic  24.2 us (7%)
    pallas_call x3, Pallas kernels, grid_product(): pl.pallas_call(grid_kernel, grid=(fields // 6,), in_specs=[per_group] + [...  49.2 us
    pallas_call x3, Pallas kernels, synthesis(): pl.pallas_call(functools.partial(synthesis_kernel, slots=slots), grid_spe...  40.2 us
    pallas_call x3, Pallas kernels, analysis(): pl.pallas_call(functools.partial(analysis_kernel, slots=slots), grid_spec...  39.5 us
    pallas_call x2, Pallas kernels, legendre_table(): pl.pallas_call(functools.partial(table_kernel, lead=-(-slots // CHUNK_ROW...  31.1 us
    all_to_all x3, waiting for transfers between devices, shards_by_level(): exchange(after(tendency.reshape(2 * count, TESTS * 3, 2, width), *last))  28.7 us
    pallas_call x3, Pallas kernels, pack_level(): pl.pallas_call(pack_kernel, grid=(targets,), in_specs=[pl.BlockSpec((piec...  16.3 us
    all_to_all x2, starting transfers between devices, shards_by_level(): specs.append(exchange(after(packed, *last)))  12.9 us
    ppermute x2, starting transfers between devices, shards_by_level(): pieces.append(lax.ppermute(block, ('k', 'ma'), route))  12.4 us
  transfers between devices with their start and end apart: 16, of which 4 were waited for; matrix products, arithmetic and copies ran while one was open for 13% of the time, Pallas kernels for 55%

profile of v2, /device:TPU:0, one launch (start us, length us, event | category | flops | bytes accessed | tf_op | source)
XLA Modules:
  0.0 332.6 jit_solution(10896023566002594920)
XLA Ops:
  10.7 5.4 %pack.3 = bf16[8,6,2,8224]{3,2,1,0:T(2,128)(2,1)} custom-call(bf16[6,8,3,2,8224]{4,3,2,1,0:T(2,128)(2,1)} %bitcast.78), custom_call_target="tpu_custom_call" | custom-call | flops 5000000000 | bytes 5000000 | tf_op jit(solution)/shard_map/pack/pallas_call | solution.py:533
  16.1 4.3 %all-to-all-start = ((bf16[8,6,2,8224]{3,2,1,0:T(2,128)(2,1)}), bf16[8,6,2,8224]{3,2,1,0:T(2,128)(2,1)}, u32[]{:S(2)}, u32[]{:S(2)}) async-start(bf16[8,6,2,8224]{3,2,1,0:T(2,128)(2,1)} %pack.3), calls=%async_computation | async-start | bytes 3194880 | tf_op jit(solution)/shard_map/all_to_all | solution.py:609
  21.6 5.4 %pack.5 = bf16[8,6,2,8224]{3,2,1,0:T(2,128)(2,1)} custom-call(bf16[6,8,3,2,8224]{4,3,2,1,0:T(2,128)(2,1)} %bitcast.79), custom_call_target="tpu_custom_call" | custom-call | flops 5000000000 | bytes 5000000 | tf_op jit(solution)/shard_map/pack/pallas_call | solution.py:533
  27.0 5.4 %pack.4 = bf16[8,6,2,8224]{3,2,1,0:T(2,128)(2,1)} custom-call(bf16[6,8,3,2,8224]{4,3,2,1,0:T(2,128)(2,1)} %bitcast.80), custom_call_target="tpu_custom_call" | custom-call | flops 5000000000 | bytes 5000000 | tf_op jit(solution)/shard_map/pack/pallas_call | solution.py:533
  37.2 11.7 %collective-permute-start.4 = (bf16[3,3,96,768]{3,2,1,0:T(8,128)(2,1)}, bf16[3,3,96,768]{3,2,1,0:T(8,128)(2,1)}, u32[]{:S(2)}, u32[]{:S(2)}) collective-permute-start(bf16[3,3,96,768]{3,2,1,0:T(8,128)(2,1)} %bitcast.86), channel_id=1, source_target_pairs={{0,0},{1,1},{2,4},{3,5},{4,2},{5,3},{6,6},{7,7},{8,8},{9,9},{10,12... | collective-permute-start | bytes 3981320 | tf_op jit(solution)/shard_map/ppermute | solution.py:625
  66.5 15.5 %table.2._ = bf16[128,288,256]{2,1,0:T(8,128)(2,1)} custom-call(f32[18,128,16]{2,1,0:T(8,128)} %get-tuple-element.34.upper, f32[18,128,16]{2,1,0:T(8,128)} %get-tuple-element.33.lower, s32[128,256]{1,0:T(8,128)} %broadcast_in_dim.69.first, s32[128,256]{1,0:T(8,128)} %broadcast_in_dim.70.second, f32[128,256]{1,0:T(8,128)} %get-tuple-element.53.seed_low, ...), custom_call_target="tpu_custom_call" | custom-call | flops 20000000000 | bytes 20000000 | tf_op jit(solution)/shard_map/table/pallas_call | solution.py:282
  82.0 15.6 %table.3 = bf16[128,288,256]{2,1,0:T(8,128)(2,1)} custom-call(f32[18,128,16]{2,1,0:T(8,128)} %get-tuple-element.34.upper, f32[18,128,16]{2,1,0:T(8,128)} %get-tuple-element.33.lower, s32[128,256]{1,0:T(8,128)} %broadcast_in_dim.69.first, s32[128,256]{1,0:T(8,128)} %broadcast_in_dim.70.second, ...), custom_call_target="tpu_custom_call", output_to_operand_aliasing={{}: (7, {})} | custom-call | flops 20000000000 | bytes 20000000 | tf_op jit(solution)/shard_map/table/pallas_call | solution.py:282
  104.7 9.3 %all-to-all-start.1 = ((bf16[8,6,2,8224]{3,2,1,0:T(2,128)(2,1)}), bf16[8,6,2,8224]{3,2,1,0:T(2,128)(2,1)}, u32[]{:S(2)}, u32[]{:S(2)}) async-start(bf16[8,6,2,8224]{3,2,1,0:T(2,128)(2,1)} %pack.5), calls=%async_computation.1 | async-start | bytes 3194880 | tf_op jit(solution)/shard_map/all_to_all | solution.py:667
  114.0 13.4 %synthesis.3.spectra = bf16[24,256,384]{2,1,0:T(8,128)(2,1)} custom-call(s32[128]{0:T(128)} %get-tuple-element.60.switch, bf16[2,4,6,2,8224]{4,3,2,1,0:T(2,128)(2,1)} %bitcast.7.spec, bf16[128,288,256]{2,1,0:T(8,128)(2,1)} %table.3, f32[24,1]{1,0:T(8,128)} %get-tuple-element.37.forcing), custom_call_target="tpu_custom_call" | custom-call | flops 14000000000 | bytes 14000000 | tf_op jit(solution)/shard_map/synthesis/pallas_call | solution.py:374
  134.0 16.4 %grid_product.3.fourier = bf16[24,256,384]{2,1,0:T(8,128)(2,1)} custom-call(bf16[24,256,384]{2,1,0:T(8,128)(2,1)} %synthesis.3.spectra, bf16[2,3,96,768]{3,2,1,0:T(8,128)(2,1)} %bitcast.19.first, bf16[2,3,96,768]{3,2,1,0:T(8,128)(2,1)} %select_bitcast_fusion.second, bf16[384,384]{1,0:T(8,128)(2,1)} %compare_convert_fusion.arrange, ...), custom_call_target="tpu_custom_call" | custom-call | flops 16000000000 | bytes 16000000 | tf_op jit(solution)/shard_map/grid_product/pallas_call | solution.py:438
  155.6 13.2 %analysis.3 = bf16[2,4,6,2,8224]{4,3,2,1,0:T(2,128)(2,1)} custom-call(s32[128]{0:T(128)} %get-tuple-element.60.switch, bf16[24,256,384]{2,1,0:T(8,128)(2,1)} %grid_product.3.fourier, bf16[128,288,256]{2,1,0:T(8,128)(2,1)} %table.3), custom_call_target="tpu_custom_call" | custom-call | flops 14000000000 | bytes 14000000 | tf_op jit(solution)/shard_map/analysis/pallas_call | solution.py:509
  173.1 13.4 %synthesis.4.spectra = bf16[24,256,384]{2,1,0:T(8,128)(2,1)} custom-call(s32[128]{0:T(128)} %get-tuple-element.60.switch, bf16[2,4,6,2,8224]{4,3,2,1,0:T(2,128)(2,1)} %bitcast.34.spec, bf16[128,288,256]{2,1,0:T(8,128)(2,1)} %table.3, f32[24,1]{1,0:T(8,128)} %get-tuple-element.36.forcing), custom_call_target="tpu_custom_call" | custom-call | flops 14000000000 | bytes 14000000 | tf_op jit(solution)/shard_map/synthesis/pallas_call | solution.py:374
  186.5 6.9 %all-to-all-done.2 = bf16[8,6,2,8224]{3,2,1,0:T(2,128)(2,1)S(1)} async-done(((bf16[8,6,2,8224]{3,2,1,0:T(2,128)(2,1)}), bf16[8,6,2,8224]{3,2,1,0:T(2,128)(2,1)S(1)}, u32[]{:S(2)}, u32[]{:S(2)}) %all-to-all-start.2) | async-done | bytes 1579040 | tf_op jit(solution)/shard_map/all_to_all | solution.py:667
  198.1 16.4 %grid_product.4.fourier = bf16[24,256,384]{2,1,0:T(8,128)(2,1)} custom-call(bf16[24,256,384]{2,1,0:T(8,128)(2,1)} %synthesis.4.spectra, bf16[2,3,96,768]{3,2,1,0:T(8,128)(2,1)} %get-tuple-element.26.first, bf16[2,3,96,768]{3,2,1,0:T(8,128)(2,1)} %get-tuple-element.24.second, bf16[384,384]{1,0:T(8,128)(2,1)} %compare_convert_fusion.arrange, ...), custom_call_target="tpu_custom_call" | custom-call | flops 16000000000 | bytes 16000000 | tf_op jit(solution)/shard_map/grid_product/pallas_call | solution.py:438
  214.5 13.2 %analysis.4 = bf16[2,4,6,2,8224]{4,3,2,1,0:T(2,128)(2,1)} custom-call(s32[128]{0:T(128)} %get-tuple-element.60.switch, bf16[24,256,384]{2,1,0:T(8,128)(2,1)} %grid_product.4.fourier, bf16[128,288,256]{2,1,0:T(8,128)(2,1)} %table.3), custom_call_target="tpu_custom_call" | custom-call | flops 14000000000 | bytes 14000000 | tf_op jit(solution)/shard_map/analysis/pallas_call | solution.py:509
  227.7 13.4 %synthesis.5.spectra = bf16[24,256,384]{2,1,0:T(8,128)(2,1)} custom-call(s32[128]{0:T(128)} %get-tuple-element.60.switch, bf16[2,4,6,2,8224]{4,3,2,1,0:T(2,128)(2,1)} %bitcast.82, bf16[128,288,256]{2,1,0:T(8,128)(2,1)} %table.3, f32[24,1]{1,0:T(8,128)} %get-tuple-element.35.forcing), custom_call_target="tpu_custom_call" | custom-call | flops 14000000000 | bytes 14000000 | tf_op jit(solution)/shard_map/synthesis/pallas_call | solution.py:374
  242.3 5.0 %all-to-all-start.4 = ((bf16[8,6,2,8224]{3,2,1,0:T(2,128)(2,1)}), bf16[8,6,2,8224]{3,2,1,0:T(2,128)(2,1)S(1)}, u32[]{:S(2)}, u32[]{:S(2)}) async-start(bf16[8,6,2,8224]{3,2,1,0:T(2,128)(2,1)} %bitcast.84), calls=%async_computation.4 | async-start | bytes 3194880 | tf_op jit(solution)/shard_map/all_to_all | solution.py:677
  247.3 16.4 %grid_product.5.fourier = bf16[24,256,384]{2,1,0:T(8,128)(2,1)} custom-call(bf16[24,256,384]{2,1,0:T(8,128)(2,1)} %synthesis.5.spectra, bf16[2,3,96,768]{3,2,1,0:T(8,128)(2,1)} %get-tuple-element.25.first, bf16[2,3,96,768]{3,2,1,0:T(8,128)(2,1)} %get-tuple-element.23.second, bf16[384,384]{1,0:T(8,128)(2,1)} %compare_convert_fusion.arrange, ...), custom_call_target="tpu_custom_call" | custom-call | flops 16000000000 | bytes 16000000 | tf_op jit(solution)/shard_map/grid_product/pallas_call | solution.py:438
  263.7 13.1 %analysis.5 = bf16[2,4,6,2,8224]{4,3,2,1,0:T(2,128)(2,1)} custom-call(s32[128]{0:T(128)} %get-tuple-element.60.switch, bf16[24,256,384]{2,1,0:T(8,128)(2,1)} %grid_product.5.fourier, bf16[128,288,256]{2,1,0:T(8,128)(2,1)} %table.3), custom_call_target="tpu_custom_call" | custom-call | flops 14000000000 | bytes 14000000 | tf_op jit(solution)/shard_map/analysis/pallas_call | solution.py:509
  276.9 8.3 %all-to-all-done.4 = bf16[8,6,2,8224]{3,2,1,0:T(2,128)(2,1)S(1)} async-done(((bf16[8,6,2,8224]{3,2,1,0:T(2,128)(2,1)}), bf16[8,6,2,8224]{3,2,1,0:T(2,128)(2,1)S(1)}, u32[]{:S(2)}, u32[]{:S(2)}) %all-to-all-start.4) | async-done | bytes 1579040 | tf_op jit(solution)/shard_map/all_to_all | solution.py:677
  290.0 10.1 %fusion.base = f32[2,3,2,4,3,2,8224]{6,5,4,3,2,1,0:T(2,128)} fusion(f32[2,3,2,4,3,2,8224]{6,5,4,3,2,1,0:T(2,128)} %bitcast.74, bf16[2,3,2,4,3,2,8224]{6,5,4,3,2,1,0:T(2,128)(2,1)} %bitcast.81, f32[8224]{0:T(1024)S(1)} %copy-done.6), kind=kLoop, calls=%fused_computation.1 | loop fusion | flops 7105536 | bytes 23718016 | tf_op jit(solution)/shard_map/sub | solution.py:648
  300.1 3.7 %finish.3.base = f32[2,3,2,4,3,2,8224]{6,5,4,3,2,1,0:T(2,128)} custom-call(f32[2,3,2,4,3,2,8224]{6,5,4,3,2,1,0:T(2,128)} %fusion.base, bf16[2,4,6,2,8224]{4,3,2,1,0:T(2,128)(2,1)} %bitcast.75), custom_call_target="tpu_custom_call", output_to_operand_aliasing={{}: (0, {})} | custom-call | flops 5000000000 | bytes 5000000 | tf_op jit(solution)/shard_map/finish/pallas_call | solution.py:557
  303.7 3.7 %finish.4.base = f32[2,3,2,4,3,2,8224]{6,5,4,3,2,1,0:T(2,128)} custom-call(f32[2,3,2,4,3,2,8224]{6,5,4,3,2,1,0:T(2,128)} %finish.3.base, bf16[2,4,6,2,8224]{4,3,2,1,0:T(2,128)(2,1)} %bitcast.76), custom_call_target="tpu_custom_call", output_to_operand_aliasing={{}: (0, {})} | custom-call | flops 5000000000 | bytes 5000000 | tf_op jit(solution)/shard_map/finish/pallas_call | solution.py:557
  307.4 20.4 %all-to-all-done.5 = bf16[8,6,2,8224]{3,2,1,0:T(2,128)(2,1)S(1)} async-done(((bf16[8,6,2,8224]{3,2,1,0:T(2,128)(2,1)}), bf16[8,6,2,8224]{3,2,1,0:T(2,128)(2,1)S(1)}, u32[]{:S(2)}, u32[]{:S(2)}) %all-to-all-start.5) | async-done | bytes 1579040 | tf_op jit(solution)/shard_map/all_to_all | solution.py:677
  (115 shorter events, 70.9 us)
Async XLA Ops:
  0.0 52.6 %collective-permute-start = (s32[32]{0:T(128)}, s32[32]{0:T(128)S(1)}, u32[]{:S(2)}, u32[]{:S(2)}) collective-permute-start(s32[32]{0:T(128)} %param.8), channel_id=1, source_target_pairs={{0,1},{1,2},{2,3},{3,0},{4,5},{5,6},{6,7},{7,4},{8,9},{9,10},{10,1... | collective-permute-start | bytes 392 | tf_op jit(solution)/shard_map/ppermute | solution.py:579
  3.0 49.6 %collective-permute-start.1 = (s32[32]{0:T(128)}, s32[32]{0:T(128)S(1)}, u32[]{:S(2)}, u32[]{:S(2)}) collective-permute-start(s32[32]{0:T(128)} %param.8), channel_id=1, source_target_pairs={{0,2},{1,3},{2,0},{3,1},{4,6},{5,7},{6,4},{7,5},{8,10},{9,11},{10,... | collective-permute-start | bytes 392 | tf_op jit(solution)/shard_map/ppermute | solution.py:579
  5.6 47.1 %collective-permute-start.2 = (s32[32]{0:T(128)}, s32[32]{0:T(128)S(1)}, u32[]{:S(2)}, u32[]{:S(2)}) collective-permute-start(s32[32]{0:T(128)} %param.8), channel_id=1, source_target_pairs={{0,3},{1,0},{2,1},{3,2},{4,7},{5,4},{6,5},{7,6},{8,11},{9,8},{10,9... | collective-permute-start | bytes 392 | tf_op jit(solution)/shard_map/ppermute | solution.py:579
  10.0 87.5 %collective-permute-start.5 = (bf16[3,3,96,768]{3,2,1,0:T(8,128)(2,1)}, bf16[3,3,96,768]{3,2,1,0:T(8,128)(2,1)S(1)}, u32[]{:S(2)}, u32[]{:S(2)}) collective-permute-start(bf16[3,3,96,768]{3,2,1,0:T(8,128)(2,1)} %bitcast.71), channel_id=1, source_target_pairs={{0,1},{1,0},{2,5},{3,4},{4,3},{5,2},{6,7},{7,6},{8,9},{9,8},{10,13... | collective-permute-start | bytes 3981320 | tf_op jit(solution)/shard_map/ppermute | solution.py:625
  16.1 86.3 %all-to-all-start = ((bf16[8,6,2,8224]{3,2,1,0:T(2,128)(2,1)}), bf16[8,6,2,8224]{3,2,1,0:T(2,128)(2,1)}, u32[]{:S(2)}, u32[]{:S(2)}) async-start(bf16[8,6,2,8224]{3,2,1,0:T(2,128)(2,1)} %pack.3), calls=%async_computation | async-start | bytes 3194880 | tf_op jit(solution)/shard_map/all_to_all | solution.py:609
  20.5 16.8 %collective-permute-start.3 = (s32[1]{0:T(128)}, s32[1]{0:T(128)}, u32[]{:S(2)}, u32[]{:S(2)}) collective-permute-start(s32[1]{0:T(128)} %param.9), channel_id=1, source_target_pairs={{0,4},{4,0},{1,5},{5,1},{2,6},{6,2},{3,7},{7,3},{8,12},{12,8},{9,1... | collective-permute-start | bytes 20 | tf_op jit(solution)/shard_map/ppermute | solution.py:599
  27.0 5.5 %copy-start.7 = (s32[32]{0:T(128)S(1)}, s32[32]{0:T(128)}, u32[]{:S(2)}) copy-start(s32[32]{0:T(128)} %param.8) | copy-start | bytes 388
  37.2 60.4 %collective-permute-start.4 = (bf16[3,3,96,768]{3,2,1,0:T(8,128)(2,1)}, bf16[3,3,96,768]{3,2,1,0:T(8,128)(2,1)}, u32[]{:S(2)}, u32[]{:S(2)}) collective-permute-start(bf16[3,3,96,768]{3,2,1,0:T(8,128)(2,1)} %bitcast.86), channel_id=1, source_target_pairs={{0,0},{1,1},{2,4},{3,5},{4,2},{5,3},{6,6},{7,7},{8,8},{9,9},{10,12... | collective-permute-start | bytes 3981320 | tf_op jit(solution)/shard_map/ppermute | solution.py:625
  97.6 1.1 copy-start.4
  99.7 1.3 copy-start.5
  102.5 24.9 %collective-permute-start.6 = (bf16[1,2,3,96,768]{4,3,2,1,0:T(8,128)(2,1)S(1)}, bf16[1,2,3,96,768]{4,3,2,1,0:T(8,128)(2,1)}, u32[]{:S(2)}, u32[]{:S(2)}) collective-permute-start(bf16[1,2,3,96,768]{4,3,2,1,0:T(8,128)(2,1)S(1)} %pad_maximum_fusion.2), channel_id=1, source_target_pairs={{0,8},{4,0},{8,12},{12,4},{1,9},{5,1},{9,13},{13,5},{2,10},{6,2},{... | collective-permute-start | bytes 2654216 | tf_op jit(solution)/shard_map/ppermute | solution.py:655
  104.0 23.4 %collective-permute-start.7 = (bf16[1,2,3,96,768]{4,3,2,1,0:T(8,128)(2,1)S(1)}, bf16[1,2,3,96,768]{4,3,2,1,0:T(8,128)(2,1)S(1)}, u32[]{:S(2)}, u32[]{:S(2)}) collective-permute-start(bf16[1,2,3,96,768]{4,3,2,1,0:T(8,128)(2,1)S(1)} %pad_maximum_fusion.2), channel_id=1, source_target_pairs={{4,8},{8,4},{5,9},{9,5},{6,10},{10,6},{7,11},{11,7},{20,24},{24,20... | collective-permute-start | bytes 2654216 | tf_op jit(solution)/shard_map/ppermute | solution.py:656
  104.7 47.3 %all-to-all-start.1 = ((bf16[8,6,2,8224]{3,2,1,0:T(2,128)(2,1)}), bf16[8,6,2,8224]{3,2,1,0:T(2,128)(2,1)}, u32[]{:S(2)}, u32[]{:S(2)}) async-start(bf16[8,6,2,8224]{3,2,1,0:T(2,128)(2,1)} %pack.5), calls=%async_computation.1 | async-start | bytes 3194880 | tf_op jit(solution)/shard_map/all_to_all | solution.py:667
  127.4 41.3 %collective-permute-start.9 = (bf16[2,2,3,96,768]{4,3,2,1,0:T(8,128)(2,1)S(1)}, bf16[2,2,3,96,768]{4,3,2,1,0:T(8,128)(2,1)}, u32[]{:S(2)}, u32[]{:S(2)}) collective-permute-start(bf16[2,2,3,96,768]{4,3,2,1,0:T(8,128)(2,1)S(1)} %pad_maximum_fusion), channel_id=1, source_target_pairs={{4,8},{8,4},{5,9},{9,5},{6,10},{10,6},{7,11},{11,7},{20,24},{24,20... | collective-permute-start | bytes 5308424 | tf_op jit(solution)/shard_map/ppermute | solution.py:656
  129.3 41.0 %collective-permute-start.8 = (bf16[2,2,3,96,768]{4,3,2,1,0:T(8,128)(2,1)S(1)}, bf16[2,2,3,96,768]{4,3,2,1,0:T(8,128)(2,1)}, u32[]{:S(2)}, u32[]{:S(2)}) collective-permute-start(bf16[2,2,3,96,768]{4,3,2,1,0:T(8,128)(2,1)S(1)} %pad_maximum_fusion), channel_id=1, source_target_pairs={{0,8},{4,0},{8,12},{12,4},{1,9},{5,1},{9,13},{13,5},{2,10},{6,2},{... | collective-permute-start | bytes 5308424 | tf_op jit(solution)/shard_map/ppermute | solution.py:655
  152.0 41.4 %all-to-all-start.2 = ((bf16[8,6,2,8224]{3,2,1,0:T(2,128)(2,1)}), bf16[8,6,2,8224]{3,2,1,0:T(2,128)(2,1)S(1)}, u32[]{:S(2)}, u32[]{:S(2)}) async-start(bf16[8,6,2,8224]{3,2,1,0:T(2,128)(2,1)} %pack.4), calls=%async_computation.2 | async-start | bytes 3194880 | tf_op jit(solution)/shard_map/all_to_all | solution.py:667
  193.4 1.2 copy-start.3
  194.5 46.6 %all-to-all-start.3 = ((bf16[8,6,2,8224]{3,2,1,0:T(2,128)(2,1)}), bf16[8,6,2,8224]{3,2,1,0:T(2,128)(2,1)S(1)}, u32[]{:S(2)}, u32[]{:S(2)}) async-start(bf16[8,6,2,8224]{3,2,1,0:T(2,128)(2,1)} %bitcast.83), calls=%async_computation.3 | async-start | bytes 3194880 | tf_op jit(solution)/shard_map/all_to_all | solution.py:677
  241.1 1.2 copy-start
  242.3 42.9 %all-to-all-start.4 = ((bf16[8,6,2,8224]{3,2,1,0:T(2,128)(2,1)}), bf16[8,6,2,8224]{3,2,1,0:T(2,128)(2,1)S(1)}, u32[]{:S(2)}, u32[]{:S(2)}) async-start(bf16[8,6,2,8224]{3,2,1,0:T(2,128)(2,1)} %bitcast.84), calls=%async_computation.4 | async-start | bytes 3194880 | tf_op jit(solution)/shard_map/all_to_all | solution.py:677
  285.2 1.2 copy-start.1
  285.2 4.8 %copy-start.6 = (f32[8224]{0:T(1024)S(1)}, f32[8224]{0:T(1024)}, u32[]{:S(2)}) copy-start(f32[8224]{0:T(1024)} %fusion.34) | copy-start | bytes 98692
  286.4 41.4 %all-to-all-start.5 = ((bf16[8,6,2,8224]{3,2,1,0:T(2,128)(2,1)}), bf16[8,6,2,8224]{3,2,1,0:T(2,128)(2,1)S(1)}, u32[]{:S(2)}, u32[]{:S(2)}) async-start(bf16[8,6,2,8224]{3,2,1,0:T(2,128)(2,1)} %bitcast.85), calls=%async_computation.5 | async-start | bytes 3194880 | tf_op jit(solution)/shard_map/all_to_all | solution.py:677
  327.8 1.2 copy-start.2

commit v3 on v2

--- a/solution.py
+++ b/solution.py
@@ -175,7 +175,7 @@
 VMEM_CAP = 56 << 20
 PAIR_ROWS = NM + 1
 CHUNK_ROWS = 16
-TABLE_PAIRS = 16
+TABLE_PAIRS = 32
 SLOTS = 16
 
 

time: 335 us -> 335 us (level)
  starting transfers between devices: 56.8 us -> 60.4 us
    all_to_all x2, starting transfers between devices: 12.9 us -> 16.5 us  [shards_by_level(): specs.append(exchange(after(packed, *last)))]
    pallas_call x2, Pallas kernels: 31.1 us -> 27.5 us  [legendre_table(): pl.pallas_call(functools.partial(table_kernel, lead=-(-slots // CHUNK_ROW...]
  transfers between devices with their start and end apart: 16 -> 16, of which waited for: 4 -> 4; matrix products, arithmetic and copies ran while one was open for 13% -> 13% of each run, Pallas kernels for 55% -> 54%
where the time goes in v3:
time: 335 us; the launch traced here: 333 us
  Pallas kernels  184 us (55%)
  starting transfers between devices  60.4 us (18%)
  waiting for transfers between devices  37.2 us (11%)
  local copies, waits for them, and re-layouts  25 us (7%)
  other arithmetic  24.2 us (7%)
    pallas_call x3, Pallas kernels, grid_product(): pl.pallas_call(grid_kernel, grid=(fields // 6,), in_specs=[per_group] + [...  49.2 us
    pallas_call x3, Pallas kernels, synthesis(): pl.pallas_call(functools.partial(synthesis_kernel, slots=slots), grid_spe...  40.2 us
    pallas_call x3, Pallas kernels, analysis(): pl.pallas_call(functools.partial(analysis_kernel, slots=slots), grid_spec...  39.5 us
    all_to_all x3, waiting for transfers between devices, shards_by_level(): exchange(after(tendency.reshape(2 * count, TESTS * 3, 2, width), *last))  28.7 us
    pallas_call x2, Pallas kernels, legendre_table(): pl.pallas_call(functools.partial(table_kernel, lead=-(-slots // CHUNK_ROW...  27.5 us
    all_to_all x2, starting transfers between devices, shards_by_level(): specs.append(exchange(after(packed, *last)))  16.5 us
    pallas_call x3, Pallas kernels, pack_level(): pl.pallas_call(pack_kernel, grid=(targets,), in_specs=[pl.BlockSpec((piec...  16.3 us
    ppermute x2, starting transfers between devices, shards_by_level(): pieces.append(lax.ppermute(block, ('k', 'ma'), route))  12.4 us
  transfers between devices with their start and end apart: 16, of which 4 were waited for; matrix products, arithmetic and copies ran while one was open for 13% of the time, Pallas kernels for 54%

profile of v3, /device:TPU:0, one launch (start us, length us, event | category | flops | bytes accessed | tf_op | source)
XLA Modules:
  0.0 332.6 jit_solution(9755850275577707198)
XLA Ops:
  10.7 5.4 %pack.3 = bf16[8,6,2,8224]{3,2,1,0:T(2,128)(2,1)} custom-call(bf16[6,8,3,2,8224]{4,3,2,1,0:T(2,128)(2,1)} %bitcast.78), custom_call_target="tpu_custom_call" | custom-call | flops 5000000000 | bytes 5000000 | tf_op jit(solution)/shard_map/pack/pallas_call | solution.py:533
  16.1 4.3 %all-to-all-start = ((bf16[8,6,2,8224]{3,2,1,0:T(2,128)(2,1)}), bf16[8,6,2,8224]{3,2,1,0:T(2,128)(2,1)}, u32[]{:S(2)}, u32[]{:S(2)}) async-start(bf16[8,6,2,8224]{3,2,1,0:T(2,128)(2,1)} %pack.3), calls=%async_computation | async-start | bytes 3194880 | tf_op jit(solution)/shard_map/all_to_all | solution.py:609
  21.6 5.4 %pack.5 = bf16[8,6,2,8224]{3,2,1,0:T(2,128)(2,1)} custom-call(bf16[6,8,3,2,8224]{4,3,2,1,0:T(2,128)(2,1)} %bitcast.79), custom_call_target="tpu_custom_call" | custom-call | flops 5000000000 | bytes 5000000 | tf_op jit(solution)/shard_map/pack/pallas_call | solution.py:533
  27.0 5.4 %pack.4 = bf16[8,6,2,8224]{3,2,1,0:T(2,128)(2,1)} custom-call(bf16[6,8,3,2,8224]{4,3,2,1,0:T(2,128)(2,1)} %bitcast.80), custom_call_target="tpu_custom_call" | custom-call | flops 5000000000 | bytes 5000000 | tf_op jit(solution)/shard_map/pack/pallas_call | solution.py:533
  37.2 11.7 %collective-permute-start.4 = (bf16[3,3,96,768]{3,2,1,0:T(8,128)(2,1)}, bf16[3,3,96,768]{3,2,1,0:T(8,128)(2,1)}, u32[]{:S(2)}, u32[]{:S(2)}) collective-permute-start(bf16[3,3,96,768]{3,2,1,0:T(8,128)(2,1)} %bitcast.86), channel_id=1, source_target_pairs={{0,0},{1,1},{2,4},{3,5},{4,2},{5,3},{6,6},{7,7},{8,8},{9,9},{10,12... | collective-permute-start | bytes 3981320 | tf_op jit(solution)/shard_map/ppermute | solution.py:625
  66.5 13.8 %table.2._ = bf16[128,288,256]{2,1,0:T(8,128)(2,1)} custom-call(f32[18,128,16]{2,1,0:T(8,128)} %get-tuple-element.34.upper, f32[18,128,16]{2,1,0:T(8,128)} %get-tuple-element.33.lower, s32[128,256]{1,0:T(8,128)} %broadcast_in_dim.69.first, s32[128,256]{1,0:T(8,128)} %broadcast_in_dim.70.second, f32[128,256]{1,0:T(8,128)} %get-tuple-element.53.seed_low, ...), custom_call_target="tpu_custom_call" | custom-call | flops 20000000000 | bytes 20000000 | tf_op jit(solution)/shard_map/table/pallas_call | solution.py:282
  80.2 13.7 %table.3 = bf16[128,288,256]{2,1,0:T(8,128)(2,1)} custom-call(f32[18,128,16]{2,1,0:T(8,128)} %get-tuple-element.34.upper, f32[18,128,16]{2,1,0:T(8,128)} %get-tuple-element.33.lower, s32[128,256]{1,0:T(8,128)} %broadcast_in_dim.69.first, s32[128,256]{1,0:T(8,128)} %broadcast_in_dim.70.second, ...), custom_call_target="tpu_custom_call", output_to_operand_aliasing={{}: (7, {})} | custom-call | flops 20000000000 | bytes 20000000 | tf_op jit(solution)/shard_map/table/pallas_call | solution.py:282
  101.1 12.9 %all-to-all-start.1 = ((bf16[8,6,2,8224]{3,2,1,0:T(2,128)(2,1)}), bf16[8,6,2,8224]{3,2,1,0:T(2,128)(2,1)}, u32[]{:S(2)}, u32[]{:S(2)}) async-start(bf16[8,6,2,8224]{3,2,1,0:T(2,128)(2,1)} %pack.5), calls=%async_computation.1 | async-start | bytes 3194880 | tf_op jit(solution)/shard_map/all_to_all | solution.py:667
  114.0 13.4 %synthesis.3.spectra = bf16[24,256,384]{2,1,0:T(8,128)(2,1)} custom-call(s32[128]{0:T(128)} %get-tuple-element.60.switch, bf16[2,4,6,2,8224]{4,3,2,1,0:T(2,128)(2,1)} %bitcast.7.spec, bf16[128,288,256]{2,1,0:T(8,128)(2,1)} %table.3, f32[24,1]{1,0:T(8,128)} %get-tuple-element.37.forcing), custom_call_target="tpu_custom_call" | custom-call | flops 14000000000 | bytes 14000000 | tf_op jit(solution)/shard_map/synthesis/pallas_call | solution.py:374
  134.0 16.4 %grid_product.3.fourier = bf16[24,256,384]{2,1,0:T(8,128)(2,1)} custom-call(bf16[24,256,384]{2,1,0:T(8,128)(2,1)} %synthesis.3.spectra, bf16[2,3,96,768]{3,2,1,0:T(8,128)(2,1)} %bitcast.19.first, bf16[2,3,96,768]{3,2,1,0:T(8,128)(2,1)} %select_bitcast_fusion.second, bf16[384,384]{1,0:T(8,128)(2,1)} %compare_convert_fusion.arrange, ...), custom_call_target="tpu_custom_call" | custom-call | flops 16000000000 | bytes 16000000 | tf_op jit(solution)/shard_map/grid_product/pallas_call | solution.py:438
  155.6 13.2 %analysis.3 = bf16[2,4,6,2,8224]{4,3,2,1,0:T(2,128)(2,1)} custom-call(s32[128]{0:T(128)} %get-tuple-element.60.switch, bf16[24,256,384]{2,1,0:T(8,128)(2,1)} %grid_product.3.fourier, bf16[128,288,256]{2,1,0:T(8,128)(2,1)} %table.3), custom_call_target="tpu_custom_call" | custom-call | flops 14000000000 | bytes 14000000 | tf_op jit(solution)/shard_map/analysis/pallas_call | solution.py:509
  173.1 13.4 %synthesis.4.spectra = bf16[24,256,384]{2,1,0:T(8,128)(2,1)} custom-call(s32[128]{0:T(128)} %get-tuple-element.60.switch, bf16[2,4,6,2,8224]{4,3,2,1,0:T(2,128)(2,1)} %bitcast.34.spec, bf16[128,288,256]{2,1,0:T(8,128)(2,1)} %table.3, f32[24,1]{1,0:T(8,128)} %get-tuple-element.36.forcing), custom_call_target="tpu_custom_call" | custom-call | flops 14000000000 | bytes 14000000 | tf_op jit(solution)/shard_map/synthesis/pallas_call | solution.py:374
  186.5 6.9 %all-to-all-done.2 = bf16[8,6,2,8224]{3,2,1,0:T(2,128)(2,1)S(1)} async-done(((bf16[8,6,2,8224]{3,2,1,0:T(2,128)(2,1)}), bf16[8,6,2,8224]{3,2,1,0:T(2,128)(2,1)S(1)}, u32[]{:S(2)}, u32[]{:S(2)}) %all-to-all-start.2) | async-done | bytes 1579040 | tf_op jit(solution)/shard_map/all_to_all | solution.py:667
  198.1 16.4 %grid_product.4.fourier = bf16[24,256,384]{2,1,0:T(8,128)(2,1)} custom-call(bf16[24,256,384]{2,1,0:T(8,128)(2,1)} %synthesis.4.spectra, bf16[2,3,96,768]{3,2,1,0:T(8,128)(2,1)} %get-tuple-element.26.first, bf16[2,3,96,768]{3,2,1,0:T(8,128)(2,1)} %get-tuple-element.24.second, bf16[384,384]{1,0:T(8,128)(2,1)} %compare_convert_fusion.arrange, ...), custom_call_target="tpu_custom_call" | custom-call | flops 16000000000 | bytes 16000000 | tf_op jit(solution)/shard_map/grid_product/pallas_call | solution.py:438
  214.5 13.2 %analysis.4 = bf16[2,4,6,2,8224]{4,3,2,1,0:T(2,128)(2,1)} custom-call(s32[128]{0:T(128)} %get-tuple-element.60.switch, bf16[24,256,384]{2,1,0:T(8,128)(2,1)} %grid_product.4.fourier, bf16[128,288,256]{2,1,0:T(8,128)(2,1)} %table.3), custom_call_target="tpu_custom_call" | custom-call | flops 14000000000 | bytes 14000000 | tf_op jit(solution)/shard_map/analysis/pallas_call | solution.py:509
  227.7 13.4 %synthesis.5.spectra = bf16[24,256,384]{2,1,0:T(8,128)(2,1)} custom-call(s32[128]{0:T(128)} %get-tuple-element.60.switch, bf16[2,4,6,2,8224]{4,3,2,1,0:T(2,128)(2,1)} %bitcast.82, bf16[128,288,256]{2,1,0:T(8,128)(2,1)} %table.3, f32[24,1]{1,0:T(8,128)} %get-tuple-element.35.forcing), custom_call_target="tpu_custom_call" | custom-call | flops 14000000000 | bytes 14000000 | tf_op jit(solution)/shard_map/synthesis/pallas_call | solution.py:374
  242.3 5.0 %all-to-all-start.4 = ((bf16[8,6,2,8224]{3,2,1,0:T(2,128)(2,1)}), bf16[8,6,2,8224]{3,2,1,0:T(2,128)(2,1)S(1)}, u32[]{:S(2)}, u32[]{:S(2)}) async-start(bf16[8,6,2,8224]{3,2,1,0:T(2,128)(2,1)} %bitcast.84), calls=%async_computation.4 | async-start | bytes 3194880 | tf_op jit(solution)/shard_map/all_to_all | solution.py:677
  247.3 16.4 %grid_product.5.fourier = bf16[24,256,384]{2,1,0:T(8,128)(2,1)} custom-call(bf16[24,256,384]{2,1,0:T(8,128)(2,1)} %synthesis.5.spectra, bf16[2,3,96,768]{3,2,1,0:T(8,128)(2,1)} %get-tuple-element.25.first, bf16[2,3,96,768]{3,2,1,0:T(8,128)(2,1)} %get-tuple-element.23.second, bf16[384,384]{1,0:T(8,128)(2,1)} %compare_convert_fusion.arrange, ...), custom_call_target="tpu_custom_call" | custom-call | flops 16000000000 | bytes 16000000 | tf_op jit(solution)/shard_map/grid_product/pallas_call | solution.py:438
  263.7 13.1 %analysis.5 = bf16[2,4,6,2,8224]{4,3,2,1,0:T(2,128)(2,1)} custom-call(s32[128]{0:T(128)} %get-tuple-element.60.switch, bf16[24,256,384]{2,1,0:T(8,128)(2,1)} %grid_product.5.fourier, bf16[128,288,256]{2,1,0:T(8,128)(2,1)} %table.3), custom_call_target="tpu_custom_call" | custom-call | flops 14000000000 | bytes 14000000 | tf_op jit(solution)/shard_map/analysis/pallas_call | solution.py:509
  276.9 8.3 %all-to-all-done.4 = bf16[8,6,2,8224]{3,2,1,0:T(2,128)(2,1)S(1)} async-done(((bf16[8,6,2,8224]{3,2,1,0:T(2,128)(2,1)}), bf16[8,6,2,8224]{3,2,1,0:T(2,128)(2,1)S(1)}, u32[]{:S(2)}, u32[]{:S(2)}) %all-to-all-start.4) | async-done | bytes 1579040 | tf_op jit(solution)/shard_map/all_to_all | solution.py:677
  290.0 10.1 %fusion.base = f32[2,3,2,4,3,2,8224]{6,5,4,3,2,1,0:T(2,128)} fusion(f32[2,3,2,4,3,2,8224]{6,5,4,3,2,1,0:T(2,128)} %bitcast.74, bf16[2,3,2,4,3,2,8224]{6,5,4,3,2,1,0:T(2,128)(2,1)} %bitcast.81, f32[8224]{0:T(1024)S(1)} %copy-done.6), kind=kLoop, calls=%fused_computation.1 | loop fusion | flops 7105536 | bytes 23718016 | tf_op jit(solution)/shard_map/sub | solution.py:648
  300.1 3.7 %finish.3.base = f32[2,3,2,4,3,2,8224]{6,5,4,3,2,1,0:T(2,128)} custom-call(f32[2,3,2,4,3,2,8224]{6,5,4,3,2,1,0:T(2,128)} %fusion.base, bf16[2,4,6,2,8224]{4,3,2,1,0:T(2,128)(2,1)} %bitcast.75), custom_call_target="tpu_custom_call", output_to_operand_aliasing={{}: (0, {})} | custom-call | flops 5000000000 | bytes 5000000 | tf_op jit(solution)/shard_map/finish/pallas_call | solution.py:557
  303.7 3.7 %finish.4.base = f32[2,3,2,4,3,2,8224]{6,5,4,3,2,1,0:T(2,128)} custom-call(f32[2,3,2,4,3,2,8224]{6,5,4,3,2,1,0:T(2,128)} %finish.3.base, bf16[2,4,6,2,8224]{4,3,2,1,0:T(2,128)(2,1)} %bitcast.76), custom_call_target="tpu_custom_call", output_to_operand_aliasing={{}: (0, {})} | custom-call | flops 5000000000 | bytes 5000000 | tf_op jit(solution)/shard_map/finish/pallas_call | solution.py:557
  307.4 20.4 %all-to-all-done.5 = bf16[8,6,2,8224]{3,2,1,0:T(2,128)(2,1)S(1)} async-done(((bf16[8,6,2,8224]{3,2,1,0:T(2,128)(2,1)}), bf16[8,6,2,8224]{3,2,1,0:T(2,128)(2,1)S(1)}, u32[]{:S(2)}, u32[]{:S(2)}) %all-to-all-start.5) | async-done | bytes 1579040 | tf_op jit(solution)/shard_map/all_to_all | solution.py:677
  (115 shorter events, 70.9 us)
Async XLA Ops:
  0.0 52.6 %collective-permute-start = (s32[32]{0:T(128)}, s32[32]{0:T(128)S(1)}, u32[]{:S(2)}, u32[]{:S(2)}) collective-permute-start(s32[32]{0:T(128)} %param.8), channel_id=1, source_target_pairs={{0,1},{1,2},{2,3},{3,0},{4,5},{5,6},{6,7},{7,4},{8,9},{9,10},{10,1... | collective-permute-start | bytes 392 | tf_op jit(solution)/shard_map/ppermute | solution.py:579
  3.0 49.6 %collective-permute-start.1 = (s32[32]{0:T(128)}, s32[32]{0:T(128)S(1)}, u32[]{:S(2)}, u32[]{:S(2)}) collective-permute-start(s32[32]{0:T(128)} %param.8), channel_id=1, source_target_pairs={{0,2},{1,3},{2,0},{3,1},{4,6},{5,7},{6,4},{7,5},{8,10},{9,11},{10,... | collective-permute-start | bytes 392 | tf_op jit(solution)/shard_map/ppermute | solution.py:579
  5.6 47.1 %collective-permute-start.2 = (s32[32]{0:T(128)}, s32[32]{0:T(128)S(1)}, u32[]{:S(2)}, u32[]{:S(2)}) collective-permute-start(s32[32]{0:T(128)} %param.8), channel_id=1, source_target_pairs={{0,3},{1,0},{2,1},{3,2},{4,7},{5,4},{6,5},{7,6},{8,11},{9,8},{10,9... | collective-permute-start | bytes 392 | tf_op jit(solution)/shard_map/ppermute | solution.py:579
  10.0 83.9 %collective-permute-start.5 = (bf16[3,3,96,768]{3,2,1,0:T(8,128)(2,1)}, bf16[3,3,96,768]{3,2,1,0:T(8,128)(2,1)S(1)}, u32[]{:S(2)}, u32[]{:S(2)}) collective-permute-start(bf16[3,3,96,768]{3,2,1,0:T(8,128)(2,1)} %bitcast.71), channel_id=1, source_target_pairs={{0,1},{1,0},{2,5},{3,4},{4,3},{5,2},{6,7},{7,6},{8,9},{9,8},{10,13... | collective-permute-start | bytes 3981320 | tf_op jit(solution)/shard_map/ppermute | solution.py:625
  16.1 82.7 %all-to-all-start = ((bf16[8,6,2,8224]{3,2,1,0:T(2,128)(2,1)}), bf16[8,6,2,8224]{3,2,1,0:T(2,128)(2,1)}, u32[]{:S(2)}, u32[]{:S(2)}) async-start(bf16[8,6,2,8224]{3,2,1,0:T(2,128)(2,1)} %pack.3), calls=%async_computation | async-start | bytes 3194880 | tf_op jit(solution)/shard_map/all_to_all | solution.py:609
  20.5 16.8 %collective-permute-start.3 = (s32[1]{0:T(128)}, s32[1]{0:T(128)}, u32[]{:S(2)}, u32[]{:S(2)}) collective-permute-start(s32[1]{0:T(128)} %param.9), channel_id=1, source_target_pairs={{0,4},{4,0},{1,5},{5,1},{2,6},{6,2},{3,7},{7,3},{8,12},{12,8},{9,1... | collective-permute-start | bytes 20 | tf_op jit(solution)/shard_map/ppermute | solution.py:599
  27.0 5.5 %copy-start.7 = (s32[32]{0:T(128)S(1)}, s32[32]{0:T(128)}, u32[]{:S(2)}) copy-start(s32[32]{0:T(128)} %param.8) | copy-start | bytes 388
  37.2 56.8 %collective-permute-start.4 = (bf16[3,3,96,768]{3,2,1,0:T(8,128)(2,1)}, bf16[3,3,96,768]{3,2,1,0:T(8,128)(2,1)}, u32[]{:S(2)}, u32[]{:S(2)}) collective-permute-start(bf16[3,3,96,768]{3,2,1,0:T(8,128)(2,1)} %bitcast.86), channel_id=1, source_target_pairs={{0,0},{1,1},{2,4},{3,5},{4,2},{5,3},{6,6},{7,7},{8,8},{9,9},{10,12... | collective-permute-start | bytes 3981320 | tf_op jit(solution)/shard_map/ppermute | solution.py:625
  94.0 1.1 copy-start.4
  96.1 1.3 copy-start.5
  98.9 28.5 %collective-permute-start.6 = (bf16[1,2,3,96,768]{4,3,2,1,0:T(8,128)(2,1)S(1)}, bf16[1,2,3,96,768]{4,3,2,1,0:T(8,128)(2,1)}, u32[]{:S(2)}, u32[]{:S(2)}) collective-permute-start(bf16[1,2,3,96,768]{4,3,2,1,0:T(8,128)(2,1)S(1)} %pad_maximum_fusion.2), channel_id=1, source_target_pairs={{0,8},{4,0},{8,12},{12,4},{1,9},{5,1},{9,13},{13,5},{2,10},{6,2},{... | collective-permute-start | bytes 2654216 | tf_op jit(solution)/shard_map/ppermute | solution.py:655
  100.4 27.0 %collective-permute-start.7 = (bf16[1,2,3,96,768]{4,3,2,1,0:T(8,128)(2,1)S(1)}, bf16[1,2,3,96,768]{4,3,2,1,0:T(8,128)(2,1)S(1)}, u32[]{:S(2)}, u32[]{:S(2)}) collective-permute-start(bf16[1,2,3,96,768]{4,3,2,1,0:T(8,128)(2,1)S(1)} %pad_maximum_fusion.2), channel_id=1, source_target_pairs={{4,8},{8,4},{5,9},{9,5},{6,10},{10,6},{7,11},{11,7},{20,24},{24,20... | collective-permute-start | bytes 2654216 | tf_op jit(solution)/shard_map/ppermute | solution.py:656
  101.1 50.9 %all-to-all-start.1 = ((bf16[8,6,2,8224]{3,2,1,0:T(2,128)(2,1)}), bf16[8,6,2,8224]{3,2,1,0:T(2,128)(2,1)}, u32[]{:S(2)}, u32[]{:S(2)}) async-start(bf16[8,6,2,8224]{3,2,1,0:T(2,128)(2,1)} %pack.5), calls=%async_computation.1 | async-start | bytes 3194880 | tf_op jit(solution)/shard_map/all_to_all | solution.py:667
  127.4 41.3 %collective-permute-start.9 = (bf16[2,2,3,96,768]{4,3,2,1,0:T(8,128)(2,1)S(1)}, bf16[2,2,3,96,768]{4,3,2,1,0:T(8,128)(2,1)}, u32[]{:S(2)}, u32[]{:S(2)}) collective-permute-start(bf16[2,2,3,96,768]{4,3,2,1,0:T(8,128)(2,1)S(1)} %pad_maximum_fusion), channel_id=1, source_target_pairs={{4,8},{8,4},{5,9},{9,5},{6,10},{10,6},{7,11},{11,7},{20,24},{24,20... | collective-permute-start | bytes 5308424 | tf_op jit(solution)/shard_map/ppermute | solution.py:656
  129.3 41.0 %collective-permute-start.8 = (bf16[2,2,3,96,768]{4,3,2,1,0:T(8,128)(2,1)S(1)}, bf16[2,2,3,96,768]{4,3,2,1,0:T(8,128)(2,1)}, u32[]{:S(2)}, u32[]{:S(2)}) collective-permute-start(bf16[2,2,3,96,768]{4,3,2,1,0:T(8,128)(2,1)S(1)} %pad_maximum_fusion), channel_id=1, source_target_pairs={{0,8},{4,0},{8,12},{12,4},{1,9},{5,1},{9,13},{13,5},{2,10},{6,2},{... | collective-permute-start | bytes 5308424 | tf_op jit(solution)/shard_map/ppermute | solution.py:655
  152.0 41.4 %all-to-all-start.2 = ((bf16[8,6,2,8224]{3,2,1,0:T(2,128)(2,1)}), bf16[8,6,2,8224]{3,2,1,0:T(2,128)(2,1)S(1)}, u32[]{:S(2)}, u32[]{:S(2)}) async-start(bf16[8,6,2,8224]{3,2,1,0:T(2,128)(2,1)} %pack.4), calls=%async_computation.2 | async-start | bytes 3194880 | tf_op jit(solution)/shard_map/all_to_all | solution.py:667
  193.4 1.2 copy-start.3
  194.5 46.6 %all-to-all-start.3 = ((bf16[8,6,2,8224]{3,2,1,0:T(2,128)(2,1)}), bf16[8,6,2,8224]{3,2,1,0:T(2,128)(2,1)S(1)}, u32[]{:S(2)}, u32[]{:S(2)}) async-start(bf16[8,6,2,8224]{3,2,1,0:T(2,128)(2,1)} %bitcast.83), calls=%async_computation.3 | async-start | bytes 3194880 | tf_op jit(solution)/shard_map/all_to_all | solution.py:677
  241.1 1.2 copy-start
  242.3 42.9 %all-to-all-start.4 = ((bf16[8,6,2,8224]{3,2,1,0:T(2,128)(2,1)}), bf16[8,6,2,8224]{3,2,1,0:T(2,128)(2,1)S(1)}, u32[]{:S(2)}, u32[]{:S(2)}) async-start(bf16[8,6,2,8224]{3,2,1,0:T(2,128)(2,1)} %bitcast.84), calls=%async_computation.4 | async-start | bytes 3194880 | tf_op jit(solution)/shard_map/all_to_all | solution.py:677
  285.2 1.2 copy-start.1
  285.2 4.8 %copy-start.6 = (f32[8224]{0:T(1024)S(1)}, f32[8224]{0:T(1024)}, u32[]{:S(2)}) copy-start(f32[8224]{0:T(1024)} %fusion.34) | copy-start | bytes 98692
  286.4 41.4 %all-to-all-start.5 = ((bf16[8,6,2,8224]{3,2,1,0:T(2,128)(2,1)}), bf16[8,6,2,8224]{3,2,1,0:T(2,128)(2,1)S(1)}, u32[]{:S(2)}, u32[]{:S(2)}) async-start(bf16[8,6,2,8224]{3,2,1,0:T(2,128)(2,1)} %bitcast.85), calls=%async_computation.5 | async-start | bytes 3194880 | tf_op jit(solution)/shard_map/all_to_all | solution.py:677
  327.8 1.2 copy-start.2
